TPU v7x, 128 devices: a whole 4x4x4 slice. The times are simulated.
128 devices in a mesh: head: 4 (over y), req: 32 (over x, z, core).
Axes of the slice: x: 4, y: 4, z: 4, core: 2. Of those that a mesh axis runs over, the one named last changes fastest.
Arguments:
- hidden_in: bfloat16 [512, 2048], P('req'), may hold values from -40 to 40
- gain_attn: float32 [2048], replicated, may hold values from 0.1 to 1.9
- gain_moe: float32 [2048], replicated, may hold values from 0.1 to 1.9
- w_query: bfloat16 [2048, 2048], P(None, 'head'), may hold values from -0.125 to 0.125
- w_key: bfloat16 [2048, 2048], P(None, 'head'), may hold values from -0.125 to 0.125
- w_value: bfloat16 [2048, 2048], P(None, 'head'), may hold values from -0.125 to 0.125
- w_out: bfloat16 [2048, 2048], P('head'), may hold values from -0.47851562 to 0.47851562
- w_router: bfloat16 [2048, 64], replicated, may hold values from -32 to 32
- w_gate: bfloat16 [64, 2048, 1024], P('req', None, 'head'), may hold values from -0.125 to 0.125
- w_up: bfloat16 [64, 2048, 1024], P('req', None, 'head'), may hold values from -0.125 to 0.125
- w_down: bfloat16 [64, 1024, 2048], P('req', 'head'), may hold values from -1.5 to 1.5
- cache_kv: bfloat16 [2, 256, 256, 2048], P(None, 'req', None, 'head'), may hold values from -210 to 210
- parked_kv: bfloat16 [2, 256, 256, 2048], P(None, 'req', None, 'head'), may hold values from -210 to 210
- lengths: int32 [512], replicated, may hold values from 1 to 256, 65536 in all
- cache_source: int32 [256], replicated, may hold values from 0 to 255, each once
- expert_ids: int32 [512, 8], P('req'), may hold values from 0 to 63, all different within a row; in each aligned block of 16 rows (0 to 15, 16 to 31, ...) at most 4 rows name the same one
Outputs:
- layer_out: bfloat16 [512, 2048], P('req', 'head')
Inputs may be any that keep to these rules, and one draw needn't show every extreme that they name: `cache_source`: every parked row belongs to exactly one continuing request. `expert_ids`: in each aligned block of 16 rows no expert is named by more than 4 rows, a bound that some block reaches.
All inputs are finite; a program needn't handle non-finite values.
Results may differ from a plain program's by a relative error of at most 0.025.
Values may be sent and summed in bfloat16 or wider, within the bound.
A program may use at most 128 MiB of HBM per device.

v0:
```python
import jax
import jax.numpy as jnp
from jax import lax
from jax.sharding import PartitionSpec as P

D = 2048
H = 16
E = 64


epsilon = 1e-06
rope_base = 50000.0


def rms_scale(inputs, gain):
    inputs = inputs.astype(jnp.float32)
    inverse = lax.rsqrt(jnp.mean(inputs * inputs, axis=-1, keepdims=True) + epsilon)
    return inputs * inverse * gain


def rotate(vectors, positions):
    half_dim = vectors.shape[-1] // 2
    frequency = rope_base ** (-2.0 * jnp.arange(half_dim, dtype=jnp.float32) / vectors.shape[-1])
    angles = positions.astype(jnp.float32)[:, None] * frequency[None, :]
    cosine = jnp.cos(angles)[:, None, :]
    sine_part = jnp.sin(angles)[:, None, :]
    leading = vectors[..., :half_dim]
    trailing = vectors[..., half_dim:]
    return jnp.concatenate(
        [leading * cosine - trailing * sine_part, trailing * cosine + leading * sine_part], axis=-1
    )


def cache_block(queries, cache_rows, row_lengths):
    item_count, span_len = (cache_rows.shape[1], cache_rows.shape[2])
    heads_here, head_dim = (queries.shape[1], queries.shape[2])
    key_rows = cache_rows[0].reshape(item_count, span_len, heads_here, head_dim)
    value_rows = cache_rows[1].reshape(item_count, span_len, heads_here, head_dim)
    scores = jnp.einsum(
        "nhd,njhd->nhj", queries, key_rows, preferred_element_type=jnp.float32
    ) * head_dim ** (-0.5)
    usable = (jnp.arange(span_len, dtype=jnp.int32)[None, :] < row_lengths[:, None])[:, None, :]
    scores = jnp.where(usable, scores, -1e30)
    row_max = jnp.max(scores, axis=-1)
    weights = jnp.where(usable, jnp.exp(scores - row_max[:, :, None]), 0.0)
    row_total = jnp.sum(weights, axis=-1)
    weighted = jnp.einsum(
        "nhj,njhd->nhd",
        weights.astype(jnp.bfloat16),
        value_rows,
        preferred_element_type=jnp.float32,
    )
    return (weighted, row_max, row_total)


def finish(weighted, row_max, row_total, queries, key_new, value_new):
    new_score = jnp.sum(
        queries.astype(jnp.float32) * key_new.astype(jnp.float32), axis=-1
    ) * queries.shape[-1] ** (-0.5)
    joint_max = jnp.maximum(row_max, new_score)
    old_part = jnp.exp(row_max - joint_max)
    new_part = jnp.exp(new_score - joint_max)
    numerator = weighted * old_part[..., None] + new_part[..., None] * value_new.astype(jnp.float32)
    return numerator / (row_total * old_part + new_part)[..., None]


def slot_table(route_ids, expert_total, capacity):
    item_count, picks_per = route_ids.shape
    flat_hot = (
        route_ids.reshape(-1)[:, None] == jnp.arange(expert_total, dtype=jnp.int32)[None, :]
    ).astype(jnp.int32)
    earlier = jnp.cumsum(flat_hot, axis=0) - flat_hot
    slot_rank = jnp.sum(earlier * flat_hot, axis=1)
    slot_hot = (slot_rank[:, None] == jnp.arange(capacity, dtype=jnp.int32)[None, :]).astype(
        jnp.float32
    )
    placed = jnp.einsum("pe,pc->ecp", flat_hot.astype(jnp.float32), slot_hot)
    return placed.reshape(expert_total, capacity, item_count, picks_per).sum(axis=-1)


def body(
    hidden_in,
    gain_attn,
    gain_moe,
    w_query,
    w_key,
    w_value,
    w_out,
    w_router,
    w_gate,
    w_up,
    w_down,
    cache_kv,
    parked_kv,
    lengths,
    cache_source,
    expert_ids,
):
    row_count = hidden_in.shape[0]
    resident = cache_kv.shape[1]
    local_width = w_query.shape[1]
    head_dim = D // H
    local_heads = local_width // head_dim
    req_count = lax.axis_size("req")
    req_index = lax.axis_index("req")
    head_index = lax.axis_index("head")
    highest = lax.Precision.HIGHEST
    normed_attn = rms_scale(hidden_in, gain_attn).astype(jnp.bfloat16)
    own_lengths = lax.dynamic_slice_in_dim(lengths, req_index * row_count, row_count)
    queries = jnp.dot(normed_attn, w_query, preferred_element_type=jnp.float32).reshape(
        row_count, local_heads, head_dim
    )
    queries = rotate(queries, own_lengths).astype(jnp.bfloat16)
    key_new = jnp.dot(normed_attn, w_key, preferred_element_type=jnp.float32).reshape(
        row_count, local_heads, head_dim
    )
    key_new = rotate(key_new, own_lengths).astype(jnp.bfloat16)
    value_new = (
        jnp.dot(normed_attn, w_value, preferred_element_type=jnp.float32)
        .astype(jnp.bfloat16)
        .reshape(row_count, local_heads, head_dim)
    )
    home_weighted, home_max, home_total = cache_block(
        queries[:resident], cache_kv, own_lengths[:resident]
    )
    moving = queries[resident:].reshape(resident, local_width)
    all_moving = lax.all_gather(moving, "req", axis=0, tiled=True)
    slot_ids = req_index * resident + jnp.arange(resident, dtype=jnp.int32)
    owner_hot = cache_source[None, :] == slot_ids[:, None]
    parked_queries = jnp.dot(
        owner_hot.astype(jnp.bfloat16), all_moving, preferred_element_type=jnp.float32
    )
    parked_queries = parked_queries.astype(jnp.bfloat16).reshape(resident, local_heads, head_dim)
    moving_lengths = lengths.reshape(req_count, row_count)[:, resident:].reshape(-1)
    parked_lengths = jnp.sum(jnp.where(owner_hot, moving_lengths[None, :], 0), axis=1)
    park_weighted, park_max, park_total = cache_block(parked_queries, parked_kv, parked_lengths)
    spread = owner_hot.astype(jnp.float32).T
    sent_weighted = jnp.dot(spread, park_weighted.reshape(resident, local_width), precision=highest)
    sent_max = jnp.dot(spread, park_max, precision=highest)
    sent_total = jnp.dot(spread, park_total, precision=highest)
    back_weighted, back_max, back_total = (
        lax.psum_scatter(
            sent_weighted.astype(jnp.bfloat16), "req", scatter_dimension=0, tiled=True
        ).astype(jnp.float32),
        lax.psum_scatter(
            sent_max.astype(jnp.bfloat16), "req", scatter_dimension=0, tiled=True
        ).astype(jnp.float32),
        lax.psum_scatter(
            sent_total.astype(jnp.bfloat16), "req", scatter_dimension=0, tiled=True
        ).astype(jnp.float32),
    )
    weighted = jnp.concatenate(
        [home_weighted, back_weighted.reshape(resident, local_heads, head_dim)], axis=0
    )
    row_max = jnp.concatenate([home_max, back_max], axis=0)
    row_total = jnp.concatenate([home_total, back_total], axis=0)
    attended = (
        finish(weighted, row_max, row_total, queries, key_new, value_new)
        .astype(jnp.bfloat16)
        .reshape(row_count, local_width)
    )
    head_terms = jnp.dot(attended, w_out, preferred_element_type=jnp.float32)
    residual = hidden_in.astype(jnp.float32) + lax.psum(
        head_terms.astype(jnp.bfloat16), "head"
    ).astype(jnp.float32)
    normed_moe = rms_scale(residual, gain_moe).astype(jnp.bfloat16)
    logits = jnp.dot(normed_moe, w_router, preferred_element_type=jnp.float32)
    expert_hot = expert_ids[:, :, None] == jnp.arange(E, dtype=jnp.int32)[None, None, :]
    chosen_logits = jnp.sum(jnp.where(expert_hot, logits[:, None, :], 0.0), axis=-1)
    gate_values = jax.nn.softmax(chosen_logits, axis=-1)
    gate_table = jnp.sum(jnp.where(expert_hot, gate_values[:, :, None], 0.0), axis=1)
    capacity = row_count // 4
    slot_map = slot_table(expert_ids, E, capacity)
    mix_weights = slot_map * gate_table.T[:, None, :]
    local_experts = w_gate.shape[0]
    outgoing = jnp.einsum(
        "ecn,nd->ecd", slot_map.astype(jnp.bfloat16), normed_moe, preferred_element_type=jnp.float32
    ).astype(jnp.bfloat16)
    outgoing = outgoing.reshape(req_count, local_experts, capacity, -1)
    arrived = lax.all_to_all(outgoing, "req", split_axis=0, concat_axis=0, tiled=True)
    gate_part = jnp.einsum("secd,edf->secf", arrived, w_gate, preferred_element_type=jnp.float32)
    up_part = jnp.einsum("secd,edf->secf", arrived, w_up, preferred_element_type=jnp.float32)
    hidden = (jax.nn.silu(gate_part) * up_part).astype(jnp.bfloat16)
    partial_out = jnp.einsum("secf,efd->secd", hidden, w_down, preferred_element_type=jnp.float32)
    result = lax.all_to_all(
        partial_out.astype(jnp.bfloat16), "req", split_axis=0, concat_axis=0, tiled=True
    ).astype(partial_out.dtype)
    returned = result
    returned = returned.reshape(E, capacity, -1)
    mixture = jnp.einsum("ecn,ecd->nd", mix_weights, returned, precision=highest)
    share = lax.psum_scatter(
        mixture.astype(jnp.bfloat16), "head", scatter_dimension=1, tiled=True
    ).astype(jnp.float32)
    own_residual = lax.dynamic_slice_in_dim(
        residual, head_index * share.shape[1], share.shape[1], axis=1
    )
    return (own_residual + share).astype(jnp.bfloat16)


def solution(mesh):
    placed = (
        P("req", None),
        P(),
        P(),
        P(None, "head"),
        P(None, "head"),
        P(None, "head"),
        P("head", None),
        P(),
        P("req", None, "head"),
        P("req", None, "head"),
        P("req", "head", None),
        P(None, "req", None, "head"),
        P(None, "req", None, "head"),
        P(),
        P(),
        P("req", None),
    )
    return jax.shard_map(
        body, mesh=mesh, in_specs=placed, out_specs=P("req", "head"), check_vma=False
    )
```

profile of v0, /device:TPU:1, one launch (start us, length us, event | category | flops | bytes accessed | tf_op | source)
XLA Modules:
  0.0 267.6 jit_solution(12115318070932877573)
XLA Ops:
  6.6 1.1 fusion.40
  7.7 0.8 reshape.263
  9.4 0.9 fusion.84
  10.3 2.1 fusion.104
  12.5 2.0 fusion.106
  14.8 27.5 %all_gather.3 = bf16[256,512]{1,0:T(8,128)(2,1)S(1)} all-gather(bf16[8,512]{1,0:T(8,128)(2,1)S(1)} %bitcast.150), channel_id=1, replica_groups=mesh['head'=4,'req'=32] {'req'}, dimensions={0}, use_global_device_ids=true | all-gather | bytes 270336 | tf_op jit(solution)/shard_map/all_gather | solution.py:127
  42.5 4.6 %fusion.112 = (bf16[1,8,256,512]{3,2,1,0:T(8,128)(2,1)}, bf16[1,8,256,512]{3,2,1,0:T(8,128)(2,1)}) fusion(bf16[2,8,256,512]{3,2,1,0:T(8,128)(2,1)} %param.28), kind=kLoop, calls=%fused_computation.149 | loop fusion | bytes 8388608 | tf_op jit(solution)/shard_map/slice | solution.py:38
  47.1 4.0 %reshape_squeeze.15 = bf16[8,256,4,128]{3,2,1,0:T(4,128)(2,1)} reshape(bf16[1,8,256,512]{3,2,1,0:T(8,128)(2,1)} %get-tuple-element.14) | data formatting | bytes 4194304 | tf_op jit(solution)/shard_map/reshape;squeeze | solution.py:38
  51.0 3.9 %copy.94 = bf16[1,8,256,512]{2,3,1,0:T(8,128)(2,1)} copy(bf16[1,8,256,512]{3,2,1,0:T(8,128)(2,1)} %get-tuple-element.15) | data formatting | bytes 4194304 | tf_op jit(solution)/shard_map/reshape;squeeze | solution.py:37
  55.0 2.1 fusion.74
  57.7 1.2 convolution_convert_fusion.3
  59.8 4.6 %fusion.111 = (bf16[1,8,256,512]{3,2,1,0:T(8,128)(2,1)}, bf16[1,8,256,512]{3,2,1,0:T(8,128)(2,1)}) fusion(bf16[2,8,256,512]{3,2,1,0:T(8,128)(2,1)} %param.27), kind=kLoop, calls=%fused_computation.148 | loop fusion | bytes 8388608 | tf_op jit(solution)/shard_map/slice | solution.py:38
  64.4 4.0 %reshape_squeeze.13 = bf16[8,256,4,128]{3,2,1,0:T(4,128)(2,1)} reshape(bf16[1,8,256,512]{3,2,1,0:T(8,128)(2,1)} %get-tuple-element.12) | data formatting | bytes 4194304 | tf_op jit(solution)/shard_map/reshape;squeeze | solution.py:38
  68.4 3.9 %copy.93 = bf16[1,8,256,512]{2,3,1,0:T(8,128)(2,1)} copy(bf16[1,8,256,512]{3,2,1,0:T(8,128)(2,1)} %get-tuple-element.13) | data formatting | bytes 4194304 | tf_op jit(solution)/shard_map/reshape;squeeze | solution.py:37
  72.3 2.0 fusion.76
  76.0 2.0 fusion.9
  78.0 62.3 %all-reduce.2 = (bf16[256,4]{0,1:T(4,128)(2,1)S(1)}, bf16[256,4]{0,1:T(4,128)(2,1)S(1)}) all-reduce(bf16[256,4]{0,1:T(4,128)(2,1)S(1)} %convolution_convert_fusion.7, bf16[256,4]{0,1:T(4,128)(2,1)S(1)} %convolution_convert_fusion.6), channel_id=3, replica_groups=mesh['head'=4,'req'=32] {'req'}, use_global_device_ids=true, to_apply=%region_5.6.clone | all-reduce | flops 2048 | bytes 8192
  142.0 3.6 %convolution_convert_fusion.2 = bf16[16,2048]{1,0:T(8,128)(2,1)} fusion(bf16[512,2048]{1,0:T(8,128)(2,1)} %param.22, bf16[2048,512]{1,0:T(8,128)(2,1)} %param.21, f32[2,8,4,128]{3,2,1,0:T(4,128)S(1)} %bitcast.147, f32[2,8,4,128]{3,2,1,0:T(4,128)S(1)} %bitcast.145, f32[2,8,4,128]{3,2,1,0:T(4,128)S(1)} %bitcast.146, f32[8,512]{1,0:T(8,128)S(1)} %convert_element_type.107, ...), kind=kOutput, calls=%fused_computation.5 | convolution fusion | flops 67338240 | bytes 4464704 | tf_op jit(solution)/shard_map/dot_general | solution.py:162
  145.8 37.8 %all-reduce.5.cloned.1.call-done = bf16[16,2048]{1,0:T(8,128)(2,1)} async-done(((bf16[16,2048]{1,0:T(8,128)(2,1)}), bf16[16,2048]{1,0:T(8,128)(2,1)}) %all-reduce.5.cloned.1.call-update) | async-done | bytes 65552 | tf_op jit(solution)/shard_map/psum | solution.py:163
  183.7 1.6 convert_add_fusion
  185.3 1.3 convolution_convert_fusion.1
  186.6 0.8 copy.95
  187.4 26.4 %all_to_all.10 = bf16[32,2,4,2048]{3,2,1,0:T(4,128)(2,1)S(1)} all-to-all(bf16[32,2,4,2048]{3,2,1,0:T(4,128)(2,1)S(1)} %bitcast.144), channel_id=1, replica_groups=mesh['head'=4,'req'=32] {'req'}, dimensions={0} | all-to-all | bytes 2097152 | tf_op jit(solution)/shard_map/all_to_all | solution.py:180
  213.8 0.9 fusion.11
  214.8 3.9 %fusion = bf16[32,2,4,2048]{3,0,2,1:T(8,128)(2,1)} fusion(bf16[2,256,2048]{2,1,0:T(8,128)(2,1)S(1)} %copy-done, bf16[2,2048,256]{2,1,0:T(8,128)(2,1)} %param.25, bf16[32,2,4,2048]{3,2,1,0:T(4,128)(2,1)S(1)} %all_to_all.10, f32[32,2,4,256]{3,0,2,1:T(8,128)S(1)} %fusion.11), kind=kOutput, calls=%fused_computation.2 | convolution fusion | flops 537788416 | bytes 6553600 | tf_op jit(solution)/shard_map/secf,efd->secd/dot_general | solution.py:184
  218.7 3.1 %copy.76 = bf16[32,2,4,2048]{3,2,1,0:T(4,128)(2,1)} copy(bf16[32,2,4,2048]{3,0,2,1:T(8,128)(2,1)} %fusion) | data formatting | bytes 2097152 | tf_op jit(solution)/shard_map/convert_element_type | solution.py:186
  221.7 4.0 %all-to-all-start.1 = ((bf16[32,2,4,2048]{3,2,1,0:T(4,128)(2,1)}), bf16[32,2,4,2048]{3,2,1,0:T(4,128)(2,1)S(1)}, u32[]{:S(2)}, u32[]{:S(2)}) async-start(bf16[32,2,4,2048]{3,2,1,0:T(4,128)(2,1)} %copy.76), calls=%async_computation.2 | async-start | bytes 2097152 | tf_op jit(solution)/shard_map/all_to_all | solution.py:185
  225.7 1.2 fusion.101
  227.6 15.0 %all-to-all-done.1 = bf16[32,2,4,2048]{3,2,1,0:T(4,128)(2,1)S(1)} async-done(((bf16[32,2,4,2048]{3,2,1,0:T(4,128)(2,1)}), bf16[32,2,4,2048]{3,2,1,0:T(4,128)(2,1)S(1)}, u32[]{:S(2)}, u32[]{:S(2)}) %all-to-all-start.1) | async-done | bytes 1048608 | tf_op jit(solution)/shard_map/all_to_all | solution.py:185
  242.6 2.2 fusion.1
  244.8 14.9 %reduce-scatter.7.cloned.1.call-done = bf16[16,512]{1,0:T(8,128)(2,1)} async-done(((bf16[16,2048]{1,0:T(8,128)(2,1)}), bf16[16,512]{1,0:T(8,128)(2,1)}) %reduce-scatter.7.cloned.1.call-update) | async-done | bytes 16400 | tf_op jit(solution)/shard_map/reduce_scatter | solution.py:191
  259.7 1.4 add_convert_fusion
  (75 shorter events, 6.7 us)
Async XLA Ops:
  6.5 208.2 %copy-start = (bf16[2,256,2048]{2,1,0:T(8,128)(2,1)S(1)}, bf16[2,256,2048]{2,1,0:T(8,128)(2,1)}, u32[]{:S(2)}) copy-start(bf16[2,256,2048]{2,1,0:T(8,128)(2,1)} %param.26) | copy-start | bytes 6291460
  6.5 5.9 %copy-start.1 = (bf16[16,2048]{1,0:T(8,128)(2,1)S(1)}, bf16[16,2048]{1,0:T(8,128)(2,1)}, u32[]{:S(2)}) copy-start(bf16[16,2048]{1,0:T(8,128)(2,1)} %param.16) | copy-start | bytes 196612
  6.5 5.9 %copy-start.5 = (f32[2048]{0:T(1024)S(1)}, f32[2048]{0:T(1024)}, u32[]{:S(2)}) copy-start(f32[2048]{0:T(1024)} %param.17) | copy-start | bytes 24580
  6.5 134.5 %reduce-scatter.5.cloned.1.call-start = ((), (), s32[]{:S(2)}) async-start(), calls=%async_computation.4 | async-start | bytes 270336 | tf_op jit(solution)/shard_map/reduce_scatter | solution.py:142
  10.3 32.0 %copy-start.7 = (s32[256]{0:T(256)S(1)}, s32[256]{0:T(256)}, u32[]{:S(2)}) copy-start(s32[256]{0:T(256)} %param.30) | copy-start | bytes 3076
  55.0 2.4 copy-start.2
  55.0 4.3 %copy-start.8 = (s32[16,8]{0,1:T(8,128)S(1)}, s32[16,8]{0,1:T(8,128)}, u32[]{:S(2)}) copy-start(s32[16,8]{0,1:T(8,128)} %param.31) | copy-start | bytes 1540
  59.0 124.7 %all-reduce.5.cloned.1.call-start = ((), (), s32[]{:S(2)}) async-start(), calls=%async_computation.5 | async-start | bytes 131072 | tf_op jit(solution)/shard_map/psum | solution.py:163
  72.3 2.5 copy-start.9
  142.0 43.3 %copy-start.6 = (f32[2048]{0:T(1024)S(1)}, f32[2048]{0:T(1024)}, u32[]{:S(2)}) copy-start(f32[2048]{0:T(1024)} %param.18) | copy-start | bytes 24580
  186.6 27.2 %copy-start.3 = (bf16[2,2048,256]{2,1,0:T(8,128)(2,1)S(1)}, bf16[2,2048,256]{2,1,0:T(8,128)(2,1)}, u32[]{:S(2)}) copy-start(bf16[2,2048,256]{2,1,0:T(8,128)(2,1)} %param.24) | copy-start | bytes 6291460
  218.7 7.1 %copy-start.4 = (bf16[16,2048]{1,0:T(8,128)(2,1)S(1)}, bf16[16,2048]{1,0:T(8,128)(2,1)}, u32[]{:S(2)}) copy-start(bf16[16,2048]{1,0:T(8,128)(2,1)} %all-reduce.5.cloned.1.call-done) | copy-start | bytes 196612
  221.7 20.9 %all-to-all-start.1 = ((bf16[32,2,4,2048]{3,2,1,0:T(4,128)(2,1)}), bf16[32,2,4,2048]{3,2,1,0:T(4,128)(2,1)S(1)}, u32[]{:S(2)}, u32[]{:S(2)}) async-start(bf16[32,2,4,2048]{3,2,1,0:T(4,128)(2,1)} %copy.76), calls=%async_computation.2 | async-start | bytes 2097152 | tf_op jit(solution)/shard_map/all_to_all | solution.py:185
  225.7 34.0 %reduce-scatter.7.cloned.1.call-start = ((), (), s32[]{:S(2)}) async-start(), calls=%async_computation.6 | async-start | bytes 81920 | tf_op jit(solution)/shard_map/reduce_scatter | solution.py:191
Sparse Core Ops, SparseCore 0:
  59.1 73.8 reduce-scatter.4
  145.8 37.8 all-reduce.4
  244.9 14.7 reduce-scatter.6
where the time goes:
time: 270 us; the launch traced here: 268 us
  blocking collectives  116 us (43%)
  waiting for transfers between devices  67.8 us (25%)
  local copies, waits for them, and re-layouts  31.2 us (12%)
  matrix products  25.4 us (9%)
  between operations  14 us (5%)
  other arithmetic  9.06 us (3%)
  starting transfers between devices  4.04 us (1%)
    unnamed x1, blocking collectives  62.3 us
    psum x1, waiting for transfers between devices, body(): lax.psum(head_terms.astype(jnp.bfloat16), 'head').astype(jnp.float32)  37.8 us
    all_gather x1, blocking collectives, body(): all_moving = lax.all_gather(moving, 'req', axis=0, tiled=True)  27.5 us
    all_to_all x1, blocking collectives, body(): lax.all_to_all(outgoing, 'req', split_axis=0, concat_axis=0, tiled=True)  26.4 us
    all_to_all x1, waiting for transfers between devices, body(): lax.all_to_all(partial_out.astype(jnp.bfloat16), 'req', split_axis=0, con...  15 us
    reduce_scatter x1, waiting for transfers between devices, body(): lax.psum_scatter(mixture.astype(jnp.bfloat16), 'head', scatter_dimension=...  14.9 us
    slice x2, local copies, waits for them, and re-layouts, cache_block(): cache_rows[1].reshape(item_count, span_len, heads_here, head_dim)  9.18 us
    another operation x2, local copies, waits for them, and re-layouts, cache_block(): cache_rows[1].reshape(item_count, span_len, heads_here, head_dim)  7.94 us
  transfers between devices with their start and end apart: 4, of which 3 were waited for; matrix products, arithmetic and copies ran while one was open for 8% of the time, Pallas kernels for 0%

commit v1 on v0

v1 whole, which is shorter than its diff:
```python
import jax
import jax.numpy as jnp
import numpy as np
from jax import lax
from jax.experimental import pallas as pl
from jax.experimental.pallas import tpu as pltpu
from jax.sharding import PartitionSpec as P

MESH = pl.DeviceIdType.MESH
F32 = jnp.float32
BF16 = jnp.bfloat16
I32 = jnp.int32

D = 2048
HD = 128
E = 64
NREQ = 32
NHEAD = 4
ROWS = 16
RES = 8
SPAN = 256
WIDTH = 512
FFL = 256
SCALE = HD ** (-0.5)
EPS = 1e-06


def iota(shape, dim):
    return lax.broadcasted_iota(I32, shape, dim)


def rms_scale(x, gain):
    inverse = lax.rsqrt(jnp.mean(x * x, axis=-1, keepdims=True) + EPS)
    return x * inverse * gain


def round_trip(x):
    return x.astype(BF16).astype(F32)


def dot(a, b):
    return jnp.dot(a, b, preferred_element_type=F32)


def rotate(x, cosine, sine):
    parts = []
    for h in range(NHEAD):
        u = x[:, h * HD:(h + 1) * HD]
        parts.append(u * cosine + pltpu.roll(u, HD // 2, 1) * sine)
    return jnp.concatenate(parts, axis=1)


def cache_attention(q, row_lengths, kv):
    stacked = jnp.concatenate([q] * NHEAD, axis=0)
    row = iota((NHEAD * RES, WIDTH), 0)
    col = iota((NHEAD * RES, WIDTH), 1)
    stacked = jnp.where(row // RES == col // HD, stacked, 0.0)
    scores = jnp.zeros((NHEAD * RES, SPAN), F32)
    for i in range(RES):
        part = jnp.where(row % RES == i, stacked, 0.0).astype(BF16)
        scores = scores + lax.dot_general(
            part, kv[0, i], (((1,), (1,)), ((), ())), preferred_element_type=F32)
    scores = scores * SCALE
    limit = jnp.concatenate([row_lengths] * NHEAD, axis=0)
    usable = iota((NHEAD * RES, SPAN), 1).astype(F32) < limit
    scores = jnp.where(usable, scores, -1e30)
    row_max = jnp.max(scores, axis=1, keepdims=True)
    weights = jnp.where(usable, jnp.exp(scores - row_max), 0.0)
    row_total = jnp.sum(weights, axis=1, keepdims=True)
    probs = weights.astype(BF16)
    pieces = [jnp.zeros((RES, HD), F32)] * NHEAD
    small = iota((RES, HD), 0)
    for i in range(RES):
        out = dot(probs, kv[1, i])
        for h in range(NHEAD):
            pieces[h] = jnp.where(
                small == i, out[h * RES:(h + 1) * RES, h * HD:(h + 1) * HD], pieces[h])
    maxes = [row_max[h * RES:(h + 1) * RES] for h in range(NHEAD)]
    totals = [row_total[h * RES:(h + 1) * RES] for h in range(NHEAD)]
    normal = [pieces[h] / totals[h] for h in range(NHEAD)]
    return normal, maxes, totals


def kernel(
    hidden_ref, gain_a_ref, gain_m_ref, freq_ref, lengths_ref, source_ref, ids_ref,
    wq_hbm, wk_hbm, wv_hbm, wo_hbm, wr_hbm, wg_hbm, wu_hbm, wd_hbm, cache_hbm, parked_hbm,
    out_ref,
    wq, wk, wv, wo, wr, wg, wu, wd, cache, parked,
    q_send, q_all, a_send, a_all, head_all, disp, arrived, ret_send, ret, fin_send, fin_all, resid,
    load_sem, q_ss, q_rs, a_ss, a_rs, h_ss, h_rs, d_ss, d_rs, r_ss, r_rs, f_ss, f_rs,
):
    me = lax.axis_index("req")
    head = lax.axis_index("head")

    loads = {}
    order = [("wq", wq_hbm, wq), ("wk", wk_hbm, wk), ("wv", wv_hbm, wv), ("cache", cache_hbm, cache),
             ("parked", parked_hbm, parked), ("wo", wo_hbm, wo), ("wr", wr_hbm, wr),
             ("wg", wg_hbm, wg), ("wu", wu_hbm, wu), ("wd", wd_hbm, wd)]
    for n, (name, src, dst) in enumerate(order):
        loads[name] = pltpu.make_async_copy(src, dst, load_sem.at[n])
        loads[name].start()

    barrier = pltpu.get_barrier_semaphore()

    def hello(d, carry):
        pl.semaphore_signal(barrier, inc=1, device_id={"req": (me + d) % NREQ}, device_id_type=MESH)
        return carry

    lax.fori_loop(1, NREQ, hello, 0)
    for d in range(1, NHEAD):
        pl.semaphore_signal(barrier, inc=1, device_id={"head": (head + d) % NHEAD}, device_id_type=MESH)

    def exchange(axis, count, mine, block_of, landing, ss, rs):
        def copy(d):
            peer = (mine + d) % count
            return pltpu.make_async_remote_copy(
                src_ref=block_of(peer), dst_ref=landing.at[mine], send_sem=ss.at[d], recv_sem=rs.at[mine],
                device_id={axis: peer}, device_id_type=MESH)

        def start(d, carry):
            copy(d).start()
            return carry

        lax.fori_loop(1, count, start, 0)

        def finish_recv(d, carry):
            other = (mine + d) % count
            pltpu.make_async_remote_copy(
                src_ref=block_of(other), dst_ref=landing.at[other], send_sem=ss.at[d], recv_sem=rs.at[other],
                device_id={axis: other}, device_id_type=MESH).wait_recv()
            return carry

        def finish_send(d, carry):
            copy(d).wait_send()
            return carry

        return (lambda: lax.fori_loop(1, count, finish_recv, 0),
                lambda: lax.fori_loop(1, count, finish_send, 0))

    hidden = hidden_ref[...].astype(F32)
    normed = rms_scale(hidden, gain_a_ref[...]).astype(BF16)
    pick = iota((ROWS, NREQ * ROWS), 1) == me * ROWS + iota((ROWS, NREQ * ROWS), 0)
    own_len = jnp.sum(jnp.where(pick, lengths_ref[...].astype(F32), 0.0), axis=1, keepdims=True)
    angles = own_len * freq_ref[...]
    cosine = jnp.cos(angles)
    sine = jnp.sin(angles)
    sine = jnp.where(iota((ROWS, HD), 1) < HD // 2, -sine, sine)
    loads["wq"].wait()
    q = round_trip(rotate(dot(normed, wq[...]), cosine, sine))

    len_block = jnp.broadcast_to(own_len[RES:], (RES, HD))
    q_block = jnp.concatenate([
        jnp.concatenate([q[RES:, :256], len_block], axis=1),
        jnp.concatenate([q[RES:, 256:], len_block], axis=1)], axis=0).astype(BF16)
    q_send[...] = q_block
    q_all[me] = q_block
    pl.semaphore_wait(barrier, NREQ - 1 + NHEAD - 1)
    q_recv, q_sent = exchange("req", NREQ, me, lambda p: q_send, q_all, q_ss, q_rs)

    loads["wk"].wait()
    k = round_trip(rotate(dot(normed, wk[...]), cosine, sine))
    loads["wv"].wait()
    v = round_trip(dot(normed, wv[...]))

    wide = NREQ * ROWS
    g_row = iota((ROWS, wide), 0)
    g_col = iota((ROWS, wide), 1)
    same_half = g_row // RES == (g_col % ROWS) // RES
    spread = iota((256, wide), 0) == (iota((256, wide), 1) // ROWS) * RES + iota((256, wide), 1) % RES
    source = jnp.broadcast_to(source_ref[...].astype(F32), (RES, 256))
    source_wide = dot(source.astype(BF16), spread.astype(F32).astype(BF16))[0:1]
    hot_park = (same_half & (source_wide == (me * RES + g_row % RES).astype(F32))).astype(F32).astype(BF16)
    pick = iota((ROWS, 256), 1) == me * RES + iota((ROWS, 256), 0) % RES
    own_source = jnp.sum(jnp.where(pick, source_ref[...].astype(F32), 0.0), axis=1, keepdims=True)
    slot = ((g_col // ROWS) * RES + g_col % RES).astype(F32)
    hot_home = (same_half & (own_source == slot)).astype(F32).astype(BF16)

    loads["cache"].wait()
    home_a, home_m, home_t = cache_attention(q[:RES], own_len[:RES], cache)

    q_recv()
    parked_q = dot(hot_park, q_all[...].reshape(wide, 384))
    loads["parked"].wait()
    park_a, park_m, park_t = cache_attention(
        jnp.concatenate([parked_q[:RES, :256], parked_q[RES:, :256]], axis=1), parked_q[:RES, 256:257], parked)

    lane = iota((RES, HD), 1)
    halves = []
    for half in range(2):
        stats = jnp.zeros((RES, HD), F32)
        for w in range(2):
            m, t = park_m[2 * half + w], park_t[2 * half + w]
            m0 = round_trip(m)
            m1 = round_trip(m - m0)
            m2 = m - m0 - m1
            t0 = round_trip(t)
            t1 = t - t0
            for n, value in enumerate((m0, m1, m2, t0, t1)):
                stats = jnp.where(lane == 8 * w + n, value, stats)
        halves.append(jnp.concatenate([park_a[2 * half], park_a[2 * half + 1], stats], axis=1))
    a_block = jnp.concatenate(halves, axis=0).astype(BF16)
    a_send[...] = a_block
    a_all[me] = a_block
    a_recv, a_sent = exchange("req", NREQ, me, lambda p: a_send, a_all, a_ss, a_rs)
    q_sent()

    new_score = [SCALE * jnp.sum(q[:, h * HD:(h + 1) * HD] * k[:, h * HD:(h + 1) * HD], axis=1, keepdims=True)
                 for h in range(NHEAD)]

    ids = ids_ref[...]
    expert = iota((ROWS, E), 1)
    chosen = jnp.zeros((ROWS, E), F32)
    for n in range(ids.shape[1]):
        chosen = jnp.where(ids[:, n:n + 1] == expert, 1.0, chosen)
    lower = (iota((ROWS, ROWS), 1) < iota((ROWS, ROWS), 0)).astype(F32).astype(BF16)
    rank = dot(lower, chosen.astype(BF16))
    e_of = iota((E, wide), 0)
    w_of = iota((E, wide), 1)
    expand = (e_of == (w_of // ROWS) * 2 + (w_of % RES) // 4).astype(F32).astype(BF16)
    placed = dot(jnp.concatenate([chosen, rank], axis=0).astype(BF16), expand)
    taken = jnp.where((placed[:ROWS] > 0.5) & (placed[ROWS:] == (g_col % 4).astype(F32)), 1.0, 0.0)
    low_half = (g_col % ROWS) // RES == 0
    taken_halves = jnp.concatenate([jnp.where(low_half, taken, 0.0), jnp.where(low_half, 0.0, taken)], axis=0)
    taken_t = taken_halves.T.astype(BF16)

    a_recv()
    back = dot(hot_home, a_all[...].reshape(wide, 384))
    pieces = []
    for h in range(NHEAD):
        half, w = h // 2, h % 2
        rows = back[half * RES:(half + 1) * RES]
        st = rows[:, 256 + 8 * w:256 + 8 * w + 5]
        back_m = st[:, 0:1] + st[:, 1:2] + st[:, 2:3]
        back_t = st[:, 3:4] + st[:, 4:5]
        a = jnp.concatenate([home_a[h], rows[:, w * HD:(w + 1) * HD]], axis=0)
        m = jnp.concatenate([home_m[h], back_m], axis=0)
        t = jnp.concatenate([home_t[h], back_t], axis=0)
        top = jnp.maximum(m, new_score[h])
        old = t * jnp.exp(m - top)
        new = jnp.exp(new_score[h] - top)
        total = old + new
        pieces.append(a * (old / total) + v[:, h * HD:(h + 1) * HD] * (new / total))
    attended = jnp.concatenate(pieces, axis=1).astype(BF16)

    loads["wo"].wait()
    terms = dot(attended, wo[...]).astype(BF16)
    head_all[head] = terms
    h_recv, h_sent = exchange("head", NHEAD, head, lambda p: head_all.at[head], head_all, h_ss, h_rs)
    a_sent()
    h_recv()
    residual = hidden + ((head_all[0].astype(F32) + head_all[1].astype(F32))
                         + (head_all[2].astype(F32) + head_all[3].astype(F32)))
    resid[...] = residual
    normed_f = round_trip(rms_scale(residual, gain_m_ref[...]))

    stacked = jnp.concatenate([normed_f[:, :1024], normed_f[:, 1024:]], axis=0).astype(BF16)
    disp[...] = dot(taken_t, stacked).astype(BF16).reshape(NREQ, ROWS, 1024)
    arrived[me] = disp[me]
    d_recv, d_sent = exchange("req", NREQ, me, lambda p: disp.at[p], arrived, d_ss, d_rs)
    h_sent()

    loads["wr"].wait()
    logits = dot(normed_f.astype(BF16), wr[...])
    hit = chosen > 0.5
    top = jnp.max(jnp.where(hit, logits, -3e38), axis=1, keepdims=True)
    power = jnp.where(hit, jnp.exp(jnp.where(hit, logits, top) - top), 0.0)
    gates = power / jnp.sum(power, axis=1, keepdims=True)
    g_hi = round_trip(gates)
    gate_wide = dot(jnp.concatenate([g_hi, gates - g_hi], axis=0).astype(BF16), expand)
    mix_hi = gate_wide[:ROWS] * taken
    mix_lo = gate_wide[ROWS:] * taken
    mix = jnp.concatenate([
        jnp.where(low_half, mix_hi, 0.0), jnp.where(low_half, mix_lo, 0.0),
        jnp.where(low_half, 0.0, mix_hi), jnp.where(low_half, 0.0, mix_lo)], axis=0).astype(BF16)

    loads["wg"].wait()
    loads["wu"].wait()
    loads["wd"].wait()
    d_recv()
    tokens = arrived[...].astype(F32).reshape(NREQ, 2, RES, 1024)
    left = tokens[:, 0].reshape(NREQ * RES, 1024).astype(BF16)
    right = tokens[:, 1].reshape(NREQ * RES, 1024).astype(BF16)
    which = (iota((NREQ * RES, FFL), 0) % RES) // 4
    inner = []
    for e in range(2):
        gate = dot(left, wg[e, :1024]) + dot(right, wg[e, 1024:])
        up = dot(left, wu[e, :1024]) + dot(right, wu[e, 1024:])
        act = gate / (1.0 + jnp.exp(-gate)) * up
        inner.append(jnp.where(which == e, act, 0.0).astype(BF16))
    parts = []
    for half in range(2):
        cols = slice(half * 1024, (half + 1) * 1024)
        y = dot(inner[0], wd[0, :, cols]) + dot(inner[1], wd[1, :, cols])
        parts.append(y.reshape(NREQ, RES, 1024))
    ret_send[...] = jnp.concatenate(parts, axis=1).astype(BF16)
    ret[me] = ret_send[me]
    r_recv, r_sent = exchange("req", NREQ, me, lambda p: ret_send.at[p], ret, r_ss, r_rs)
    d_sent()
    r_recv()
    mixed = dot(mix, ret[...].reshape(wide, 1024))
    mixture = [mixed[0:16] + mixed[16:32], mixed[32:48] + mixed[48:64]]
    for h in range(NHEAD):
        fin_send[h] = mixture[h // 2][:, (h % 2) * WIDTH:(h % 2 + 1) * WIDTH].astype(BF16)
    fin_all[head] = fin_send[head]
    f_recv, f_sent = exchange("head", NHEAD, head, lambda p: fin_send.at[p], fin_all, f_ss, f_rs)
    r_sent()
    f_recv()
    own = resid[:, pl.ds(pl.multiple_of(head * WIDTH, WIDTH), WIDTH)]
    total = own + ((fin_all[0].astype(F32) + fin_all[1].astype(F32))
                   + (fin_all[2].astype(F32) + fin_all[3].astype(F32)))
    out_ref[...] = total.astype(BF16)
    f_sent()


def body(hidden_in, gain_attn, gain_moe, w_query, w_key, w_value, w_out, w_router, w_gate, w_up, w_down,
         cache_kv, parked_kv, lengths, cache_source, expert_ids):
    half = HD // 2
    freq = 50000.0 ** (-2.0 * np.arange(half, dtype=np.float64) / HD)
    freq = jnp.asarray(np.concatenate([freq, freq])[None, :], F32)
    vmem = pl.BlockSpec(memory_space=pltpu.VMEM)
    hbm = pl.BlockSpec(memory_space=pl.ANY)
    dma = pltpu.SemaphoreType.DMA
    big = [w_query, w_key, w_value, w_out, w_router, w_gate, w_up, w_down, cache_kv, parked_kv]
    block = (NREQ, ROWS, 384)
    wide = (NREQ, ROWS, 1024)
    return pl.pallas_call(
        kernel,
        out_shape=jax.ShapeDtypeStruct((ROWS, WIDTH), BF16),
        in_specs=[vmem] * 7 + [hbm] * 10,
        out_specs=vmem,
        scratch_shapes=[pltpu.VMEM(x.shape, x.dtype) for x in big] + [
            pltpu.VMEM(block[1:], BF16), pltpu.VMEM(block, BF16),
            pltpu.VMEM(block[1:], BF16), pltpu.VMEM(block, BF16),
            pltpu.VMEM((NHEAD, ROWS, D), BF16),
            pltpu.VMEM(wide, BF16), pltpu.VMEM(wide, BF16),
            pltpu.VMEM(wide, BF16), pltpu.VMEM(wide, BF16),
            pltpu.VMEM((NHEAD, ROWS, WIDTH), BF16), pltpu.VMEM((NHEAD, ROWS, WIDTH), BF16),
            pltpu.VMEM((ROWS, D), F32),
            dma((10,)),
            dma((NREQ,)), dma((NREQ,)), dma((NREQ,)), dma((NREQ,)),
            dma((NHEAD,)), dma((NHEAD,)),
            dma((NREQ,)), dma((NREQ,)), dma((NREQ,)), dma((NREQ,)),
            dma((NHEAD,)), dma((NHEAD,)),
        ],
        compiler_params=pltpu.CompilerParams(
            collective_id=0, has_side_effects=True, vmem_limit_bytes=60 * 1024 * 1024),
    )(hidden_in, gain_attn.reshape(1, D), gain_moe.reshape(1, D), freq, lengths.reshape(1, -1),
      cache_source.reshape(1, -1), expert_ids,
      w_query, w_key, w_value, w_out, w_router, w_gate, w_up, w_down, cache_kv, parked_kv)


def solution(mesh):
    placed = (
        P("req", None),
        P(),
        P(),
        P(None, "head"),
        P(None, "head"),
        P(None, "head"),
        P("head", None),
        P(),
        P("req", None, "head"),
        P("req", None, "head"),
        P("req", "head", None),
        P(None, "req", None, "head"),
        P(None, "req", None, "head"),
        P(),
        P(),
        P("req", None),
    )
    return jax.shard_map(
        body, mesh=mesh, in_specs=placed, out_specs=P("req", "head"), check_vma=False
    )
```

time: 270 us -> 79.3 us (0.29)
  blocking collectives: 116 us -> 0 us
  Pallas kernels: 0 us -> 74.4 us
  waiting for transfers between devices: 67.8 us -> 0 us
  local copies, waits for them, and re-layouts: 31.2 us -> 4.63 us
  matrix products: 25.4 us -> 0 us
  between operations: 14 us -> 0.01 us
  other arithmetic: 9.06 us -> 0 us
  starting transfers between devices: 4.04 us -> 0 us
    pallas_call x0 -> x1, Pallas kernels: none -> 74.4 us  [body(): pl.pallas_call(kernel, out_shape=jax.ShapeDtypeStruct((ROWS, WIDTH), BF16...]
    unnamed x1 -> x0, blocking collectives: 62.3 us -> none
    psum x1 -> x0, waiting for transfers between devices: 37.8 us -> none  [body(): lax.psum(head_terms.astype(jnp.bfloat16), 'head').astype(jnp.float32)]
    all_gather x1 -> x0, blocking collectives: 27.5 us -> none  [body(): all_moving = lax.all_gather(moving, 'req', axis=0, tiled=True)]
    all_to_all x1 -> x0, blocking collectives: 26.4 us -> none  [body(): lax.all_to_all(outgoing, 'req', split_axis=0, concat_axis=0, tiled=True)]
    dot_general x16 -> x0, matrix products: 25.4 us -> none  [the longest x2 4.11 us: cache_block(): jnp.einsum('nhd,njhd->nhj', queries, key_rows, preferred_element_type=jnp...]
    another operation x4 -> x0, local copies, waits for them, and re-layouts: 15.8 us -> none  [the longest x2 7.94 us: cache_block(): cache_rows[1].reshape(item_count, span_len, heads_here, head_dim)]
    all_to_all x1 -> x0, waiting for transfers between devices: 15 us -> none  [body(): lax.all_to_all(partial_out.astype(jnp.bfloat16), 'req', split_axis=0, con...]
  transfers between devices with their start and end apart: 4 -> 0, of which waited for: 3 -> 0; matrix products, arithmetic and copies ran while one was open for 8% -> 0% of each run, Pallas kernels for 0% -> 0%
where the time goes in v1:
time: 79.3 us; the launch traced here: 79 us
  Pallas kernels  74.4 us (94%)
  local copies, waits for them, and re-layouts  4.63 us (6%)
    pallas_call x1, Pallas kernels, body(): pl.pallas_call(kernel, out_shape=jax.ShapeDtypeStruct((ROWS, WIDTH), BF16...  74.4 us
    unnamed x3, local copies, waits for them, and re-layouts  4.63 us

profile of v1, /device:TPU:1, one launch (start us, length us, event | category | flops | bytes accessed | tf_op | source)
XLA Modules:
  0.0 79.0 jit_solution(10155304078432518469)
XLA Ops:
  0.0 1.4 %copy.18.ids_ref = s32[16,8]{1,0:T(8,128)} copy(s32[16,8]{0,1:T(8,128)} %param.32) | data formatting | bytes 1024 | tf_op args[15]
  1.4 1.9 %copy.19.wr_hbm = bf16[2048,64]{1,0:T(8,128)(2,1)} copy(bf16[2048,64]{0,1:T(8,128)(2,1)} %param.24) | data formatting | bytes 524288 | tf_op args[7]
  3.3 74.4 %shard_map.163 = bf16[16,512]{1,0:T(8,128)(2,1)} custom-call(bf16[16,2048]{1,0:T(8,128)(2,1)} %hidden_ref.1, f32[1,2048]{1,0:T(1,128)} %bitcast.4, f32[1,2048]{1,0:T(1,128)} %bitcast.5, f32[1,128]{1,0:T(1,128)} %constant.2.clone.freq_ref, s32[1,512]{1,0:T(1,128)} %bitcast.6, s32[1,256]{1,0:T(1,128)} %bitcast.7, s32[16,8]{1,0:T(8,128)} %copy.18.ids_ref, ...), custom_call_target="tpu_custom_call" | custom-call | tf_op jit(solution)/shard_map/pallas_call | solution.py:326
  77.7 1.3 %copy.21 = bf16[16,512]{1,0:T(8,128)(2,1)} copy(bf16[16,512]{1,0:T(8,128)(2,1)} %shard_map.163) | data formatting | bytes 32768

commit v2 on v1

v2 whole, which is shorter than its diff:
```python
import jax
import jax.numpy as jnp
import numpy as np
from jax import lax
from jax.experimental import pallas as pl
from jax.experimental.pallas import tpu as pltpu
from jax.sharding import PartitionSpec as P

MESH = pl.DeviceIdType.MESH
F32 = jnp.float32
BF16 = jnp.bfloat16
I32 = jnp.int32

D = 2048
HD = 128
E = 64
NREQ = 32
NHEAD = 4
ROWS = 16
RES = 8
SPAN = 256
WIDTH = 512
FFL = 256
SCALE = HD ** (-0.5)


def ring(step):
    return min(step, 4 - step)


OFFSETS = sorted(
    ((dx, dz, dc) for dx in range(4) for dz in range(4) for dc in range(2)),
    key=lambda o: (-(ring(o[0]) + ring(o[1])), -o[2], abs(o[0] - o[1]), o))
GROUPS = ((0, 10), (10, 22), (22, 32))
EPS = 1e-06


def iota(shape, dim):
    return lax.broadcasted_iota(I32, shape, dim)


def rms_scale(x, gain):
    inverse = lax.rsqrt(jnp.mean(x * x, axis=-1, keepdims=True) + EPS)
    return x * inverse * gain


def round_trip(x):
    return x.astype(BF16).astype(F32)


def dot(a, b):
    return jnp.dot(a, b, preferred_element_type=F32)


def rotate(x, cosine, sine):
    parts = []
    for h in range(NHEAD):
        u = x[:, h * HD:(h + 1) * HD]
        parts.append(u * cosine + pltpu.roll(u, HD // 2, 1) * sine)
    return jnp.concatenate(parts, axis=1)


def cache_attention(q, row_lengths, kv):
    stacked = jnp.concatenate([q] * NHEAD, axis=0)
    row = iota((NHEAD * RES, WIDTH), 0)
    col = iota((NHEAD * RES, WIDTH), 1)
    stacked = jnp.where(row // RES == col // HD, stacked, 0.0)
    scores = jnp.zeros((NHEAD * RES, SPAN), F32)
    for i in range(RES):
        part = jnp.where(row % RES == i, stacked, 0.0).astype(BF16)
        scores = scores + lax.dot_general(
            part, kv[0, i], (((1,), (1,)), ((), ())), preferred_element_type=F32)
    scores = scores * SCALE
    limit = jnp.concatenate([row_lengths] * NHEAD, axis=0)
    usable = iota((NHEAD * RES, SPAN), 1).astype(F32) < limit
    scores = jnp.where(usable, scores, -1e30)
    row_max = jnp.max(scores, axis=1, keepdims=True)
    weights = jnp.where(usable, jnp.exp(scores - row_max), 0.0)
    row_total = jnp.sum(weights, axis=1, keepdims=True)
    probs = weights.astype(BF16)
    pieces = [jnp.zeros((RES, HD), F32)] * NHEAD
    small = iota((RES, HD), 0)
    for i in range(RES):
        out = dot(probs, kv[1, i])
        for h in range(NHEAD):
            pieces[h] = jnp.where(
                small == i, out[h * RES:(h + 1) * RES, h * HD:(h + 1) * HD], pieces[h])
    maxes = [row_max[h * RES:(h + 1) * RES] for h in range(NHEAD)]
    totals = [row_total[h * RES:(h + 1) * RES] for h in range(NHEAD)]
    normal = [pieces[h] / totals[h] for h in range(NHEAD)]
    return normal, maxes, totals


def kernel(
    hidden_hbm, gain_a_hbm, gain_m_hbm, table_hbm, lengths_hbm, source_hbm, ids_hbm,
    wq_hbm, wk_hbm, wv_hbm, wo_hbm, wr_hbm, wg_hbm, wu_hbm, wd_hbm, cache_hbm, parked_hbm,
    out_ref,
    hidden_ref, gain_a_ref, gain_m_ref, table_ref, lengths_ref, source_ref, ids_ref,
    wq, wk, wv, wo, wr, wg, wu, wd, cache, parked,
    q_send, q_all, a_send, a_all, head_all, disp, arrived, ret_send, ret, fin_send, fin_all, resid,
    load_sem, q_ss, q_rs, a_ss, a_rs, h_ss, h_rs, d_ss, d_rs, r_ss, r_rs, f_ss, f_rs,
):
    me = lax.axis_index("req")
    head = lax.axis_index("head")
    my_x, my_z, my_c = me // 8, (me // 2) % 4, me % 2

    def ahead(n):
        dx, dz, dc = OFFSETS[n]
        return ((my_x + dx) % 4) * 8 + ((my_z + dz) % 4) * 2 + (my_c + dc) % 2

    def behind(n):
        dx, dz, dc = OFFSETS[n]
        return ((my_x + 4 - dx) % 4) * 8 + ((my_z + 4 - dz) % 4) * 2 + (my_c + dc) % 2

    barrier = pltpu.get_barrier_semaphore()
    for n in range(NREQ - 1):
        pl.semaphore_signal(barrier, inc=1, device_id={"req": ahead(n)}, device_id_type=MESH)
    for d in range(1, NHEAD):
        pl.semaphore_signal(barrier, inc=1, device_id={"head": (head + d) % NHEAD}, device_id_type=MESH)

    loads = {}
    order = [("hidden", hidden_hbm, hidden_ref), ("gain_a", gain_a_hbm, gain_a_ref),
             ("table", table_hbm, table_ref), ("lengths", lengths_hbm, lengths_ref),
             ("wq", wq_hbm, wq), ("source", source_hbm, source_ref), ("ids", ids_hbm, ids_ref),
             ("gain_m", gain_m_hbm, gain_m_ref),
             ("wk", wk_hbm, wk), ("wv", wv_hbm, wv), ("cache", cache_hbm, cache),
             ("parked", parked_hbm, parked), ("wo", wo_hbm, wo), ("wr", wr_hbm, wr),
             ("wg", wg_hbm, wg), ("wu", wu_hbm, wu), ("wd", wd_hbm, wd)]
    for n, (name, src, dst) in enumerate(order):
        loads[name] = pltpu.make_async_copy(src, dst, load_sem.at[n])
        loads[name].start()

    def launch(lo, hi, source, landing, ss, rs, target):
        hi = min(hi, NREQ - 1)
        for n in range(lo, hi):
            pltpu.make_async_remote_copy(
                src_ref=source(n), dst_ref=landing.at[n], send_sem=ss, recv_sem=rs,
                device_id={"req": target(n)}, device_id_type=MESH).start()
        whole = pltpu.make_async_remote_copy(
            src_ref=landing.at[pl.ds(lo, hi - lo)], dst_ref=landing.at[pl.ds(lo, hi - lo)],
            send_sem=ss, recv_sem=rs, device_id={"req": target(lo)}, device_id_type=MESH)
        return whole.wait_recv, whole.wait_send

    def head_exchange(source, landing, ss, rs):
        def copy(d, own):
            peer = (head + d) % NHEAD
            return pltpu.make_async_remote_copy(
                src_ref=source(peer), dst_ref=landing.at[head if own else peer], send_sem=ss.at[d],
                recv_sem=rs.at[head if own else peer], device_id={"head": peer}, device_id_type=MESH)

        for d in range(1, NHEAD):
            copy(d, True).start()

        def received():
            for d in range(1, NHEAD):
                copy(d, False).wait_recv()

        def sent():
            for d in range(1, NHEAD):
                copy(d, True).wait_send()

        return received, sent

    for name in ("hidden", "gain_a", "table", "lengths"):
        loads[name].wait()
    hidden = hidden_ref[...].astype(F32)
    normed = rms_scale(hidden, gain_a_ref[...]).astype(BF16)
    pick = iota((ROWS, NREQ * ROWS), 1) == me * ROWS + iota((ROWS, NREQ * ROWS), 0)
    lengths = lengths_ref[...].astype(F32)
    own_len = jnp.sum(jnp.where(pick, lengths, 0.0), axis=1, keepdims=True)
    angles = own_len * table_ref[0:1, :HD]
    cosine = jnp.cos(angles)
    sine = jnp.sin(angles)
    sine = jnp.where(iota((ROWS, HD), 1) < HD // 2, -sine, sine)
    loads["wq"].wait()
    q = round_trip(rotate(dot(normed, wq[...]), cosine, sine))
    q_block = jnp.concatenate([q[RES:, :256], q[RES:, 256:]], axis=0).astype(BF16)
    q_send[...] = q_block
    q_all[NREQ - 1] = q_block

    wide = NREQ * ROWS
    g_row = iota((ROWS, wide), 0)
    g_col = iota((ROWS, wide), 1)
    same_half = g_row // RES == (g_col % ROWS) // RES
    step_x = table_ref[1:2, :].astype(I32)
    step_z = table_ref[2:3, :].astype(I32)
    step_c = table_ref[3:4, :].astype(I32)
    src = ((my_x + 4 - step_x) % 4) * 8 + ((my_z + 4 - step_z) % 4) * 2 + (my_c + step_c) % 2
    dst = ((my_x + step_x) % 4) * 8 + ((my_z + step_z) % 4) * 2 + (my_c + step_c) % 2
    place = src * RES + iota((1, wide), 1) % RES
    natural = iota((256, wide), 1)
    spread = jnp.concatenate([
        (iota((256, wide), 0) == place).astype(F32),
        ((iota((256, wide), 0) == (natural // ROWS) * RES + natural % RES)
         & (natural % ROWS >= RES)).astype(F32)], axis=1).astype(BF16)
    loads["source"].wait()
    source = source_ref[...].astype(F32)
    source_wide = dot(jnp.broadcast_to(source, (RES, 256)).astype(BF16), spread)[0:1]
    hot_park = (same_half & (source_wide[:, :wide] == (me * RES + g_row % RES).astype(F32))).astype(F32).astype(BF16)
    row8 = iota((RES, wide), 0)
    hot_len = (source_wide[:, wide:] == (me * RES + row8).astype(F32)) & (iota((RES, wide), 1) % ROWS >= RES)
    park_len = jnp.sum(jnp.where(hot_len, lengths, 0.0), axis=1, keepdims=True)
    pick = iota((ROWS, 256), 1) == me * RES + iota((ROWS, 256), 0) % RES
    own_source = jnp.sum(jnp.where(pick, source, 0.0), axis=1, keepdims=True)
    hot_home = (same_half & (own_source == place.astype(F32))).astype(F32).astype(BF16)

    pl.semaphore_wait(barrier, NREQ - 1 + NHEAD - 1)
    q_recv, q_sent = launch(0, NREQ, lambda n: q_send, q_all, q_ss.at[0], q_rs.at[0], ahead)

    loads["wk"].wait()
    k = round_trip(rotate(dot(normed, wk[...]), cosine, sine))
    loads["wv"].wait()
    v = round_trip(dot(normed, wv[...]))
    loads["cache"].wait()
    home_a, home_m, home_t = cache_attention(q[:RES], own_len[:RES], cache)
    loads["parked"].wait()

    q_recv()
    parked_q = dot(hot_park, q_all[...].reshape(wide, 256))
    park_a, park_m, park_t = cache_attention(
        jnp.concatenate([parked_q[:RES], parked_q[RES:]], axis=1), park_len, parked)

    lane = iota((RES, HD), 1)
    halves = []
    for half in range(2):
        stats = jnp.zeros((RES, HD), F32)
        for w in range(2):
            m, t = park_m[2 * half + w], park_t[2 * half + w]
            m0 = round_trip(m)
            m1 = round_trip(m - m0)
            m2 = m - m0 - m1
            t0 = round_trip(t)
            t1 = t - t0
            for n, value in enumerate((m0, m1, m2, t0, t1)):
                stats = jnp.where(lane == 8 * w + n, value, stats)
        halves.append(jnp.concatenate([park_a[2 * half], park_a[2 * half + 1], stats], axis=1))
    a_block = jnp.concatenate(halves, axis=0).astype(BF16)
    a_send[...] = a_block
    a_recv, a_sent = launch(0, NREQ, lambda n: a_send, a_all, a_ss.at[0], a_rs.at[0], ahead)
    a_all[NREQ - 1] = a_block
    q_sent()

    new_score = [SCALE * jnp.sum(q[:, h * HD:(h + 1) * HD] * k[:, h * HD:(h + 1) * HD], axis=1, keepdims=True)
                 for h in range(NHEAD)]

    loads["ids"].wait()
    ids = ids_ref[...]
    expert = iota((E, ROWS), 0)
    chosen_t = jnp.zeros((E, ROWS), F32)
    for n in range(ids.shape[0]):
        chosen_t = jnp.where(ids[n:n + 1] == expert, 1.0, chosen_t)
    before = iota((ROWS, ROWS), 1) < iota((ROWS, ROWS), 0)
    same = iota((ROWS, ROWS), 1) == iota((ROWS, ROWS), 0)
    both = jnp.concatenate([same.astype(F32), before.astype(F32)], axis=0).astype(BF16)
    chosen_rank = lax.dot_general(
        both, chosen_t.astype(BF16), (((1,), (1,)), ((), ())), preferred_element_type=F32)
    chosen = chosen_rank[:ROWS]
    expand = (iota((E, wide), 0) == dst * 2 + (iota((1, wide), 1) % RES) // 4).astype(F32).astype(BF16)
    placed = dot(chosen_rank.astype(BF16), expand)
    taken = jnp.where((placed[:ROWS] > 0.5) & (placed[ROWS:] == (g_col % 4).astype(F32)), 1.0, 0.0)
    low_half = (g_col % ROWS) // RES == 0
    taken_halves = jnp.concatenate([jnp.where(low_half, taken, 0.0), jnp.where(low_half, 0.0, taken)], axis=0)
    taken_t = taken_halves.T.astype(BF16)
    loads["wo"].wait()
    loads["gain_m"].wait()

    a_recv()
    back = dot(hot_home, a_all[...].reshape(wide, 384))
    pieces = []
    for h in range(NHEAD):
        half, w = h // 2, h % 2
        rows = back[half * RES:(half + 1) * RES]
        st = rows[:, 256 + 8 * w:256 + 8 * w + 5]
        back_m = st[:, 0:1] + st[:, 1:2] + st[:, 2:3]
        back_t = st[:, 3:4] + st[:, 4:5]
        a = jnp.concatenate([home_a[h], rows[:, w * HD:(w + 1) * HD]], axis=0)
        m = jnp.concatenate([home_m[h], back_m], axis=0)
        t = jnp.concatenate([home_t[h], back_t], axis=0)
        top = jnp.maximum(m, new_score[h])
        old = t * jnp.exp(m - top)
        new = jnp.exp(new_score[h] - top)
        total = old + new
        pieces.append(a * (old / total) + v[:, h * HD:(h + 1) * HD] * (new / total))
    attended = jnp.concatenate(pieces, axis=1).astype(BF16)

    head_all[head] = dot(attended, wo[...]).astype(BF16)
    h_recv, h_sent = head_exchange(lambda p: head_all.at[head], head_all, h_ss, h_rs)
    a_sent()
    loads["wr"].wait()
    h_recv()
    residual = hidden + ((head_all[0].astype(F32) + head_all[1].astype(F32))
                         + (head_all[2].astype(F32) + head_all[3].astype(F32)))
    normed_f = round_trip(rms_scale(residual, gain_m_ref[...]))

    stacked = jnp.concatenate([normed_f[:, :1024], normed_f[:, 1024:]], axis=0).astype(BF16)
    disp[...] = dot(taken_t, stacked).astype(BF16).reshape(NREQ, ROWS, 1024)
    moves = [launch(lo, hi, lambda n: disp.at[n], arrived, d_ss.at[g], d_rs.at[g], ahead)
             for g, (lo, hi) in enumerate(GROUPS)]
    arrived[NREQ - 1] = disp[NREQ - 1]
    resid[...] = residual
    h_sent()

    logits = lax.dot_general(
        normed_f.astype(BF16), wr[...], (((1,), (1,)), ((), ())), preferred_element_type=F32)
    hit = chosen > 0.5
    top = jnp.max(jnp.where(hit, logits, -3e38), axis=1, keepdims=True)
    power = jnp.where(hit, jnp.exp(jnp.where(hit, logits, top) - top), 0.0)
    gates = power / jnp.sum(power, axis=1, keepdims=True)
    g_hi = round_trip(gates)
    gate_wide = dot(jnp.concatenate([g_hi, gates - g_hi], axis=0).astype(BF16), expand)
    mix_hi = gate_wide[:ROWS] * taken
    mix_lo = gate_wide[ROWS:] * taken
    mix = jnp.concatenate([
        jnp.where(low_half, mix_hi, 0.0), jnp.where(low_half, mix_lo, 0.0),
        jnp.where(low_half, 0.0, mix_hi), jnp.where(low_half, 0.0, mix_lo)], axis=0).astype(BF16)

    loads["wg"].wait()
    loads["wu"].wait()
    loads["wd"].wait()
    returns = []
    for g, (lo, hi) in enumerate(GROUPS):
        moves[g][0]()
        count = hi - lo
        tokens = arrived[lo:hi].astype(F32).reshape(count, 2, RES, 1024)
        left = tokens[:, 0].reshape(count * RES, 1024).astype(BF16)
        right = tokens[:, 1].reshape(count * RES, 1024).astype(BF16)
        which = (iota((count * RES, FFL), 0) % RES) // 4
        inner = []
        for e in range(2):
            gate = dot(left, wg[e, :1024]) + dot(right, wg[e, 1024:])
            up = dot(left, wu[e, :1024]) + dot(right, wu[e, 1024:])
            act = gate / (1.0 + jnp.exp(-gate)) * up
            inner.append(jnp.where(which == e, act, 0.0).astype(BF16))
        parts = []
        for half in range(2):
            cols = slice(half * 1024, (half + 1) * 1024)
            y = dot(inner[0], wd[0, :, cols]) + dot(inner[1], wd[1, :, cols])
            parts.append(y.reshape(count, RES, 1024))
        ret_send[lo:hi] = jnp.concatenate(parts, axis=1).astype(BF16)
        returns.append(launch(lo, hi, lambda n: ret_send.at[n], ret, r_ss.at[g], r_rs.at[g], behind))
    ret[NREQ - 1] = ret_send[NREQ - 1]
    for move in moves:
        move[1]()
    for back_move in returns:
        back_move[0]()
    mixed = dot(mix, ret[...].reshape(wide, 1024))
    mixture = [mixed[0:16] + mixed[16:32], mixed[32:48] + mixed[48:64]]
    for h in range(NHEAD):
        fin_send[h] = mixture[h // 2][:, (h % 2) * WIDTH:(h % 2 + 1) * WIDTH].astype(BF16)
    f_recv, f_sent = head_exchange(lambda p: fin_send.at[p], fin_all, f_ss, f_rs)
    fin_all[head] = fin_send[head]
    for back_move in returns:
        back_move[1]()
    own = resid[:, pl.ds(pl.multiple_of(head * WIDTH, WIDTH), WIDTH)]
    f_recv()
    total = own + ((fin_all[0].astype(F32) + fin_all[1].astype(F32))
                   + (fin_all[2].astype(F32) + fin_all[3].astype(F32)))
    out_ref[...] = total.astype(BF16)
    f_sent()


def body(hidden_in, gain_attn, gain_moe, w_query, w_key, w_value, w_out, w_router, w_gate, w_up, w_down,
         cache_kv, parked_kv, lengths, cache_source, expert_ids):
    half = HD // 2
    freq = 50000.0 ** (-2.0 * np.arange(half, dtype=np.float64) / HD)
    table = np.zeros((8, NREQ * ROWS), np.float32)
    table[0, :HD] = np.concatenate([freq, freq])
    table[1:4] = np.repeat(np.asarray(OFFSETS).T, ROWS, axis=1)
    hbm = pl.BlockSpec(memory_space=pl.ANY)
    dma = pltpu.SemaphoreType.DMA
    operands = [hidden_in, gain_attn.reshape(1, D), gain_moe.reshape(1, D), jnp.asarray(table),
                lengths.reshape(1, -1), cache_source.reshape(1, -1), expert_ids.T,
                w_query, w_key, w_value, w_out, w_router.T, w_gate, w_up, w_down, cache_kv, parked_kv]
    q_block = (NREQ, ROWS, 256)
    a_block = (NREQ, ROWS, 384)
    wide = (NREQ, ROWS, 1024)
    return pl.pallas_call(
        kernel,
        out_shape=jax.ShapeDtypeStruct((ROWS, WIDTH), BF16),
        in_specs=[hbm] * len(operands),
        out_specs=pl.BlockSpec(memory_space=pltpu.VMEM),
        scratch_shapes=[pltpu.VMEM(x.shape, x.dtype) for x in operands] + [
            pltpu.VMEM(q_block[1:], BF16), pltpu.VMEM(q_block, BF16),
            pltpu.VMEM(a_block[1:], BF16), pltpu.VMEM(a_block, BF16),
            pltpu.VMEM((NHEAD, ROWS, D), BF16),
            pltpu.VMEM(wide, BF16), pltpu.VMEM(wide, BF16),
            pltpu.VMEM(wide, BF16), pltpu.VMEM(wide, BF16),
            pltpu.VMEM((NHEAD, ROWS, WIDTH), BF16), pltpu.VMEM((NHEAD, ROWS, WIDTH), BF16),
            pltpu.VMEM((ROWS, D), F32),
            dma((len(operands),)),
            dma((1,)), dma((1,)), dma((1,)), dma((1,)),
            dma((NHEAD,)), dma((NHEAD,)),
            dma((len(GROUPS),)), dma((len(GROUPS),)), dma((len(GROUPS),)), dma((len(GROUPS),)),
            dma((NHEAD,)), dma((NHEAD,)),
        ],
        compiler_params=pltpu.CompilerParams(
            collective_id=0, has_side_effects=True, vmem_limit_bytes=60 * 1024 * 1024),
    )(*operands)


def solution(mesh):
    placed = (
        P("req", None),
        P(),
        P(),
        P(None, "head"),
        P(None, "head"),
        P(None, "head"),
        P("head", None),
        P(),
        P("req", None, "head"),
        P("req", None, "head"),
        P("req", "head", None),
        P(None, "req", None, "head"),
        P(None, "req", None, "head"),
        P(),
        P(),
        P("req", None),
    )
    return jax.shard_map(
        body, mesh=mesh, in_specs=placed, out_specs=P("req", "head"), check_vma=False
    )
```

time: 79.3 us -> 59.6 us (0.75)
  Pallas kernels: 74.4 us -> 58.1 us
  local copies, waits for them, and re-layouts: 4.63 us -> 1.32 us
    pallas_call x1, Pallas kernels: 74.4 us -> 58.1 us  [body(): pl.pallas_call(kernel, out_shape=jax.ShapeDtypeStruct((ROWS, WIDTH), BF16...]
    unnamed x3 -> x1, local copies, waits for them, and re-layouts: 4.63 us -> 1.32 us
where the time goes in v2:
time: 59.6 us; the launch traced here: 59.4 us
  Pallas kernels  58.1 us (97%)
  local copies, waits for them, and re-layouts  1.32 us (2%)
    pallas_call x1, Pallas kernels, body(): pl.pallas_call(kernel, out_shape=jax.ShapeDtypeStruct((ROWS, WIDTH), BF16...  58.1 us
    unnamed x1, local copies, waits for them, and re-layouts  1.32 us

profile of v2, /device:TPU:1, one launch (start us, length us, event | category | flops | bytes accessed | tf_op | source)
XLA Modules:
  0.0 59.4 jit_solution(17964536804053928022)
XLA Ops:
  0.0 58.1 %shard_map.163 = bf16[16,512]{1,0:T(8,128)(2,1)} custom-call(bf16[16,2048]{1,0:T(8,128)(2,1)} %hidden_hbm.1, f32[1,2048]{1,0:T(1,128)} %bitcast.7, f32[1,2048]{1,0:T(1,128)} %bitcast.8, f32[8,512]{1,0:T(8,128)} %constant.2.clone.table_hbm, s32[1,512]{1,0:T(1,128)} %bitcast.10, s32[1,256]{1,0:T(1,128)} %bitcast.11, s32[8,16]{1,0:T(8,128)} %bitcast.9, ...), custom_call_target="tpu_custom_call" | custom-call | tf_op jit(solution)/shard_map/pallas_call | solution.py:377
  58.1 1.3 %copy.19 = bf16[16,512]{1,0:T(8,128)(2,1)} copy(bf16[16,512]{1,0:T(8,128)(2,1)} %shard_map.163) | data formatting | bytes 32768

commit v3 on v2

--- a/solution.py
+++ b/solution.py
@@ -97,8 +97,9 @@
     out_ref,
     hidden_ref, gain_a_ref, gain_m_ref, table_ref, lengths_ref, source_ref, ids_ref,
     wq, wk, wv, wo, wr, wg, wu, wd, cache, parked,
-    q_send, q_all, a_send, a_all, head_all, disp, arrived, ret_send, ret, fin_send, fin_all, resid,
-    load_sem, q_ss, q_rs, a_ss, a_rs, h_ss, h_rs, d_ss, d_rs, r_ss, r_rs, f_ss, f_rs,
+    q_send, q_all, a_send, a_all, st_send, st_all, home_all, back_all, disp, arrived, ret_send, ret,
+    fin_send, fin_all, resid,
+    load_sem, q_ss, q_rs, a_ss, a_rs, h_ss, h_rs, d_ss, d_rs, y_ss, y_rs, r_ss, r_rs, f_ss, f_rs,
 ):
     me = lax.axis_index("req")
     head = lax.axis_index("head")
@@ -134,18 +135,19 @@
         hi = min(hi, NREQ - 1)
         for n in range(lo, hi):
             pltpu.make_async_remote_copy(
-                src_ref=source(n), dst_ref=landing.at[n], send_sem=ss, recv_sem=rs,
+                src_ref=source(n), dst_ref=landing(n), send_sem=ss, recv_sem=rs,
                 device_id={"req": target(n)}, device_id_type=MESH).start()
+        span = landing(pl.ds(lo, hi - lo))
         whole = pltpu.make_async_remote_copy(
-            src_ref=landing.at[pl.ds(lo, hi - lo)], dst_ref=landing.at[pl.ds(lo, hi - lo)],
-            send_sem=ss, recv_sem=rs, device_id={"req": target(lo)}, device_id_type=MESH)
+            src_ref=span, dst_ref=span, send_sem=ss, recv_sem=rs,
+            device_id={"req": target(lo)}, device_id_type=MESH)
         return whole.wait_recv, whole.wait_send
 
     def head_exchange(source, landing, ss, rs):
         def copy(d, own):
             peer = (head + d) % NHEAD
             return pltpu.make_async_remote_copy(
-                src_ref=source(peer), dst_ref=landing.at[head if own else peer], send_sem=ss.at[d],
+                src_ref=source(peer), dst_ref=landing(head if own else peer), send_sem=ss.at[d],
                 recv_sem=rs.at[head if own else peer], device_id={"head": peer}, device_id_type=MESH)
 
         for d in range(1, NHEAD):
@@ -202,10 +204,14 @@
     park_len = jnp.sum(jnp.where(hot_len, lengths, 0.0), axis=1, keepdims=True)
     pick = iota((ROWS, 256), 1) == me * RES + iota((ROWS, 256), 0) % RES
     own_source = jnp.sum(jnp.where(pick, source, 0.0), axis=1, keepdims=True)
+    block_src = table_ref[4:7, :3 * NREQ].astype(I32)
+    block_src = (((my_x + 4 - block_src[0:1]) % 4) * 8 + ((my_z + 4 - block_src[1:2]) % 4) * 2
+                 + (my_c + block_src[2:3]) % 2)
+    hot_block = (jnp.floor(own_source[:RES] / RES) == block_src.astype(F32)).astype(F32).astype(BF16)
     hot_home = (same_half & (own_source == place.astype(F32))).astype(F32).astype(BF16)
 
     pl.semaphore_wait(barrier, NREQ - 1 + NHEAD - 1)
-    q_recv, q_sent = launch(0, NREQ, lambda n: q_send, q_all, q_ss.at[0], q_rs.at[0], ahead)
+    q_recv, q_sent = launch(0, NREQ, lambda n: q_send, lambda n: q_all.at[n], q_ss.at[0], q_rs.at[0], ahead)
 
     loads["wk"].wait()
     k = round_trip(rotate(dot(normed, wk[...]), cosine, sine))
@@ -220,28 +226,41 @@
     park_a, park_m, park_t = cache_attention(
         jnp.concatenate([parked_q[:RES], parked_q[RES:]], axis=1), park_len, parked)
 
-    lane = iota((RES, HD), 1)
-    halves = []
-    for half in range(2):
-        stats = jnp.zeros((RES, HD), F32)
-        for w in range(2):
-            m, t = park_m[2 * half + w], park_t[2 * half + w]
-            m0 = round_trip(m)
-            m1 = round_trip(m - m0)
-            m2 = m - m0 - m1
-            t0 = round_trip(t)
-            t1 = t - t0
-            for n, value in enumerate((m0, m1, m2, t0, t1)):
-                stats = jnp.where(lane == 8 * w + n, value, stats)
-        halves.append(jnp.concatenate([park_a[2 * half], park_a[2 * half + 1], stats], axis=1))
-    a_block = jnp.concatenate(halves, axis=0).astype(BF16)
+    a_block = jnp.concatenate([
+        jnp.concatenate(park_a[:2], axis=1), jnp.concatenate(park_a[2:], axis=1)], axis=0).astype(BF16)
     a_send[...] = a_block
-    a_recv, a_sent = launch(0, NREQ, lambda n: a_send, a_all, a_ss.at[0], a_rs.at[0], ahead)
+    a_recv, a_sent = launch(0, NREQ, lambda n: a_send, lambda n: a_all.at[n], a_ss.at[0], a_rs.at[0], ahead)
+    stats = jnp.concatenate(park_m + park_t, axis=0)
+    shape = (2 * NHEAD * RES, HD)
+    stats = jnp.sum(jnp.where(iota(shape, 0) == iota(shape, 1), stats, 0.0), axis=0, keepdims=True)
+    st_send[...] = stats
+    st_recv, st_sent = launch(0, NREQ, lambda n: st_send, lambda n: st_all.at[n], a_ss.at[1], a_rs.at[1], ahead)
     a_all[NREQ - 1] = a_block
+    st_all[NREQ - 1] = stats
     q_sent()
 
     new_score = [SCALE * jnp.sum(q[:, h * HD:(h + 1) * HD] * k[:, h * HD:(h + 1) * HD], axis=1, keepdims=True)
                  for h in range(NHEAD)]
+
+    def finish(first, a, m, t):
+        pieces = []
+        for h in range(NHEAD):
+            score = new_score[h][first:first + RES]
+            top = jnp.maximum(m[h], score)
+            old = t[h] * jnp.exp(m[h] - top)
+            new = jnp.exp(score - top)
+            total = old + new
+            pieces.append(a[h] * (old / total) + v[first:first + RES, h * HD:(h + 1) * HD] * (new / total))
+        out = dot(jnp.concatenate(pieces, axis=1).astype(BF16), wo[...])
+        return jnp.concatenate([out[:, :1024], out[:, 1024:]], axis=0).astype(BF16)
+
+    def summed(parts):
+        whole = (parts[0].astype(F32) + parts[1].astype(F32)) + (parts[2].astype(F32) + parts[3].astype(F32))
+        return jnp.concatenate([whole[:RES], whole[RES:]], axis=1)
+
+    loads["wo"].wait()
+    home_all[head] = finish(0, home_a, home_m, home_t)
+    home_recv, home_sent = head_exchange(lambda p: home_all.at[head], lambda p: home_all.at[p], h_ss.at[0], h_rs.at[0])
 
     loads["ids"].wait()
     ids = ids_ref[...]
@@ -261,41 +280,43 @@
     low_half = (g_col % ROWS) // RES == 0
     taken_halves = jnp.concatenate([jnp.where(low_half, taken, 0.0), jnp.where(low_half, 0.0, taken)], axis=0)
     taken_t = taken_halves.T.astype(BF16)
-    loads["wo"].wait()
     loads["gain_m"].wait()
+    home_recv()
+    home_residual = hidden[:RES] + summed(home_all)
 
     a_recv()
-    back = dot(hot_home, a_all[...].reshape(wide, 384))
-    pieces = []
-    for h in range(NHEAD):
-        half, w = h // 2, h % 2
-        rows = back[half * RES:(half + 1) * RES]
-        st = rows[:, 256 + 8 * w:256 + 8 * w + 5]
-        back_m = st[:, 0:1] + st[:, 1:2] + st[:, 2:3]
-        back_t = st[:, 3:4] + st[:, 4:5]
-        a = jnp.concatenate([home_a[h], rows[:, w * HD:(w + 1) * HD]], axis=0)
-        m = jnp.concatenate([home_m[h], back_m], axis=0)
-        t = jnp.concatenate([home_t[h], back_t], axis=0)
-        top = jnp.maximum(m, new_score[h])
-        old = t * jnp.exp(m - top)
-        new = jnp.exp(new_score[h] - top)
-        total = old + new
-        pieces.append(a * (old / total) + v[:, h * HD:(h + 1) * HD] * (new / total))
-    attended = jnp.concatenate(pieces, axis=1).astype(BF16)
-
-    head_all[head] = dot(attended, wo[...]).astype(BF16)
-    h_recv, h_sent = head_exchange(lambda p: head_all.at[head], head_all, h_ss, h_rs)
+    back = dot(hot_home, a_all[...].reshape(wide, 256))
+    st_recv()
+    st = st_all[...].reshape(NREQ, HD)
+    st0 = round_trip(st)
+    st1 = round_trip(st - st0)
+    st = jnp.concatenate([st0, st1, st - st0 - st1], axis=0).astype(BF16)
+    picked = dot(hot_block, st)
+    lane = iota((RES, HD), 1).astype(F32)
+    turn = own_source[:RES] - jnp.floor(own_source[:RES] / RES) * RES
+    back_s = [jnp.sum(jnp.where(lane == turn + n * RES, picked, 0.0), axis=1, keepdims=True)
+              for n in range(2 * NHEAD)]
+    back_a = [back[(h // 2) * RES:(h // 2 + 1) * RES, (h % 2) * HD:(h % 2 + 1) * HD] for h in range(NHEAD)]
+    back_all[head] = finish(RES, back_a, back_s[:NHEAD], back_s[NHEAD:])
+    h_recv, h_sent = head_exchange(lambda p: back_all.at[head], lambda p: back_all.at[p], h_ss.at[1], h_rs.at[1])
     a_sent()
+    st_sent()
+    home_sent()
     loads["wr"].wait()
     h_recv()
-    residual = hidden + ((head_all[0].astype(F32) + head_all[1].astype(F32))
-                         + (head_all[2].astype(F32) + head_all[3].astype(F32)))
+    residual = jnp.concatenate([home_residual, hidden[RES:] + summed(back_all)], axis=0)
     normed_f = round_trip(rms_scale(residual, gain_m_ref[...]))
 
     stacked = jnp.concatenate([normed_f[:, :1024], normed_f[:, 1024:]], axis=0).astype(BF16)
     disp[...] = dot(taken_t, stacked).astype(BF16).reshape(NREQ, ROWS, 1024)
-    moves = [launch(lo, hi, lambda n: disp.at[n], arrived, d_ss.at[g], d_rs.at[g], ahead)
-             for g, (lo, hi) in enumerate(GROUPS)]
+    def quarter(p):
+        return pl.ds(pl.multiple_of(p * 256, 256), 256)
+
+    far = GROUPS[0][1]
+    moves = [launch(0, far, lambda n: disp.at[n, :, quarter(head)], lambda n: arrived.at[n, :, quarter(head)],
+                    d_ss.at[0], d_rs.at[0], ahead)]
+    for g, (lo, hi) in list(enumerate(GROUPS))[1:]:
+        moves.append(launch(lo, hi, lambda n: disp.at[n], lambda n: arrived.at[n], d_ss.at[g], d_rs.at[g], ahead))
     arrived[NREQ - 1] = disp[NREQ - 1]
     resid[...] = residual
     h_sent()
@@ -317,9 +338,7 @@
     loads["wg"].wait()
     loads["wu"].wait()
     loads["wd"].wait()
-    returns = []
-    for g, (lo, hi) in enumerate(GROUPS):
-        moves[g][0]()
+    def experts(lo, hi):
         count = hi - lo
         tokens = arrived[lo:hi].astype(F32).reshape(count, 2, RES, 1024)
         left = tokens[:, 0].reshape(count * RES, 1024).astype(BF16)
@@ -337,8 +356,26 @@
             y = dot(inner[0], wd[0, :, cols]) + dot(inner[1], wd[1, :, cols])
             parts.append(y.reshape(count, RES, 1024))
         ret_send[lo:hi] = jnp.concatenate(parts, axis=1).astype(BF16)
-        returns.append(launch(lo, hi, lambda n: ret_send.at[n], ret, r_ss.at[g], r_rs.at[g], behind))
+
+    def give_back(g):
+        lo, hi = GROUPS[g]
+        return launch(lo, hi, lambda n: ret_send.at[n], lambda n: ret.at[n], r_ss.at[g], r_rs.at[g], behind)
+
+    moves[0][0]()
+    y_recv, y_sent = head_exchange(
+        lambda p: arrived.at[pl.ds(0, far), :, quarter(head)],
+        lambda p: arrived.at[pl.ds(0, far), :, quarter(p)], y_ss, y_rs)
+    moves[1][0]()
+    experts(*GROUPS[1])
+    returns = [give_back(1)]
+    moves[2][0]()
+    experts(*GROUPS[2])
     ret[NREQ - 1] = ret_send[NREQ - 1]
+    y_recv()
+    experts(*GROUPS[0])
+    returns.append(give_back(0))
+    returns.append(give_back(2))
+    y_sent()
     for move in moves:
         move[1]()
     for back_move in returns:
@@ -347,7 +384,7 @@
     mixture = [mixed[0:16] + mixed[16:32], mixed[32:48] + mixed[48:64]]
     for h in range(NHEAD):
         fin_send[h] = mixture[h // 2][:, (h % 2) * WIDTH:(h % 2 + 1) * WIDTH].astype(BF16)
-    f_recv, f_sent = head_exchange(lambda p: fin_send.at[p], fin_all, f_ss, f_rs)
+    f_recv, f_sent = head_exchange(lambda p: fin_send.at[p], lambda p: fin_all.at[p], f_ss, f_rs)
     fin_all[head] = fin_send[head]
     for back_move in returns:
         back_move[1]()
@@ -366,13 +403,13 @@
     table = np.zeros((8, NREQ * ROWS), np.float32)
     table[0, :HD] = np.concatenate([freq, freq])
     table[1:4] = np.repeat(np.asarray(OFFSETS).T, ROWS, axis=1)
+    table[4:7, :3 * NREQ] = np.tile(np.asarray(OFFSETS).T, (1, 3))
     hbm = pl.BlockSpec(memory_space=pl.ANY)
     dma = pltpu.SemaphoreType.DMA
     operands = [hidden_in, gain_attn.reshape(1, D), gain_moe.reshape(1, D), jnp.asarray(table),
                 lengths.reshape(1, -1), cache_source.reshape(1, -1), expert_ids.T,
                 w_query, w_key, w_value, w_out, w_router.T, w_gate, w_up, w_down, cache_kv, parked_kv]
     q_block = (NREQ, ROWS, 256)
-    a_block = (NREQ, ROWS, 384)
     wide = (NREQ, ROWS, 1024)
     return pl.pallas_call(
         kernel,
@@ -381,16 +418,18 @@
         out_specs=pl.BlockSpec(memory_space=pltpu.VMEM),
         scratch_shapes=[pltpu.VMEM(x.shape, x.dtype) for x in operands] + [
             pltpu.VMEM(q_block[1:], BF16), pltpu.VMEM(q_block, BF16),
-            pltpu.VMEM(a_block[1:], BF16), pltpu.VMEM(a_block, BF16),
-            pltpu.VMEM((NHEAD, ROWS, D), BF16),
+            pltpu.VMEM(q_block[1:], BF16), pltpu.VMEM(q_block, BF16),
+            pltpu.VMEM((1, HD), F32), pltpu.VMEM((NREQ, 1, HD), F32),
+            pltpu.VMEM((NHEAD, ROWS, 1024), BF16), pltpu.VMEM((NHEAD, ROWS, 1024), BF16),
             pltpu.VMEM(wide, BF16), pltpu.VMEM(wide, BF16),
             pltpu.VMEM(wide, BF16), pltpu.VMEM(wide, BF16),
             pltpu.VMEM((NHEAD, ROWS, WIDTH), BF16), pltpu.VMEM((NHEAD, ROWS, WIDTH), BF16),
             pltpu.VMEM((ROWS, D), F32),
             dma((len(operands),)),
-            dma((1,)), dma((1,)), dma((1,)), dma((1,)),
-            dma((NHEAD,)), dma((NHEAD,)),
-            dma((len(GROUPS),)), dma((len(GROUPS),)), dma((len(GROUPS),)), dma((len(GROUPS),)),
+            dma((1,)), dma((1,)), dma((2,)), dma((2,)),
+            dma((2, NHEAD)), dma((2, NHEAD)),
+            dma((len(GROUPS),)), dma((len(GROUPS),)), dma((NHEAD,)), dma((NHEAD,)),
+            dma((len(GROUPS),)), dma((len(GROUPS),)),
             dma((NHEAD,)), dma((NHEAD,)),
         ],
         compiler_params=pltpu.CompilerParams(

time: 59.6 us -> 56.1 us (0.941)
  Pallas kernels: 58.1 us -> 54.5 us
    pallas_call x1, Pallas kernels: 58.1 us -> 54.5 us  [body(): pl.pallas_call(kernel, out_shape=jax.ShapeDtypeStruct((ROWS, WIDTH), BF16...]
where the time goes in v3:
time: 56.1 us; the launch traced here: 55.8 us
  Pallas kernels  54.5 us (97%)
  local copies, waits for them, and re-layouts  1.32 us (2%)
    pallas_call x1, Pallas kernels, body(): pl.pallas_call(kernel, out_shape=jax.ShapeDtypeStruct((ROWS, WIDTH), BF16...  54.5 us
    unnamed x1, local copies, waits for them, and re-layouts  1.32 us

profile of v3, /device:TPU:1, one launch (start us, length us, event | category | flops | bytes accessed | tf_op | source)
XLA Modules:
  0.0 55.8 jit_solution(3384156517473868934)
XLA Ops:
  0.0 54.5 %shard_map.163 = bf16[16,512]{1,0:T(8,128)(2,1)} custom-call(bf16[16,2048]{1,0:T(8,128)(2,1)} %hidden_hbm.1, f32[1,2048]{1,0:T(1,128)} %bitcast.7, f32[1,2048]{1,0:T(1,128)} %bitcast.8, f32[8,512]{1,0:T(8,128)} %constant.2.clone.table_hbm, s32[1,512]{1,0:T(1,128)} %bitcast.10, s32[1,256]{1,0:T(1,128)} %bitcast.11, s32[8,16]{1,0:T(8,128)} %bitcast.9, ...), custom_call_target="tpu_custom_call" | custom-call | tf_op jit(solution)/shard_map/pallas_call | solution.py:414
  54.5 1.3 %copy.19 = bf16[16,512]{1,0:T(8,128)(2,1)} copy(bf16[16,512]{1,0:T(8,128)(2,1)} %shard_map.163) | data formatting | bytes 32768

commit v4 on v3

--- a/solution.py
+++ b/solution.py
@@ -31,7 +31,9 @@
 OFFSETS = sorted(
     ((dx, dz, dc) for dx in range(4) for dz in range(4) for dc in range(2)),
     key=lambda o: (-(ring(o[0]) + ring(o[1])), -o[2], abs(o[0] - o[1]), o))
-GROUPS = ((0, 10), (10, 22), (22, 32))
+FAR = ((0, 6), (6, 10))
+NEAR = ((10, 22), (22, 32))
+FIRST = 10
 EPS = 1e-06
 
 
@@ -50,6 +52,17 @@
 
 def dot(a, b):
     return jnp.dot(a, b, preferred_element_type=F32)
+
+
+def split(x):
+    blocks = [x[:, n * 256:(n + 1) * 256] for n in range(8)]
+    return jnp.concatenate(blocks[::2], axis=1), jnp.concatenate(blocks[1::2], axis=1)
+
+
+def join(even, odd):
+    width = even.shape[1] // 256
+    return jnp.concatenate(
+        [part[:, n * 256:(n + 1) * 256] for n in range(width) for part in (even, odd)], axis=1)
 
 
 def rotate(x, cosine, sine):
@@ -98,8 +111,9 @@
     hidden_ref, gain_a_ref, gain_m_ref, table_ref, lengths_ref, source_ref, ids_ref,
     wq, wk, wv, wo, wr, wg, wu, wd, cache, parked,
     q_send, q_all, a_send, a_all, st_send, st_all, home_all, back_all, disp, arrived, ret_send, ret,
-    fin_send, fin_all, resid,
-    load_sem, q_ss, q_rs, a_ss, a_rs, h_ss, h_rs, d_ss, d_rs, y_ss, y_rs, r_ss, r_rs, f_ss, f_rs,
+    part_all, far_send, far_ret, fin_send, fin_all, resid,
+    load_sem, q_ss, q_rs, a_ss, a_rs, h_ss, h_rs, d_ss, d_rs, y_ss, y_rs, p_ss, p_rs, t_ss, t_rs,
+    r_ss, r_rs, f_ss, f_rs,
 ):
     me = lax.axis_index("req")
     head = lax.axis_index("head")
@@ -150,18 +164,11 @@
                 src_ref=source(peer), dst_ref=landing(head if own else peer), send_sem=ss.at[d],
                 recv_sem=rs.at[head if own else peer], device_id={"head": peer}, device_id_type=MESH)
 
-        for d in range(1, NHEAD):
-            copy(d, True).start()
-
-        def received():
-            for d in range(1, NHEAD):
-                copy(d, False).wait_recv()
-
-        def sent():
-            for d in range(1, NHEAD):
-                copy(d, True).wait_send()
-
-        return received, sent
+        mine = [copy(d, True) for d in range(1, NHEAD)]
+        theirs = [copy(d, False) for d in range(1, NHEAD)]
+        for move in mine:
+            move.start()
+        return (lambda: [move.wait_recv() for move in theirs]), (lambda: [move.wait_send() for move in mine])
 
     for name in ("hidden", "gain_a", "table", "lengths"):
         loads[name].wait()
@@ -210,58 +217,6 @@
     hot_block = (jnp.floor(own_source[:RES] / RES) == block_src.astype(F32)).astype(F32).astype(BF16)
     hot_home = (same_half & (own_source == place.astype(F32))).astype(F32).astype(BF16)
 
-    pl.semaphore_wait(barrier, NREQ - 1 + NHEAD - 1)
-    q_recv, q_sent = launch(0, NREQ, lambda n: q_send, lambda n: q_all.at[n], q_ss.at[0], q_rs.at[0], ahead)
-
-    loads["wk"].wait()
-    k = round_trip(rotate(dot(normed, wk[...]), cosine, sine))
-    loads["wv"].wait()
-    v = round_trip(dot(normed, wv[...]))
-    loads["cache"].wait()
-    home_a, home_m, home_t = cache_attention(q[:RES], own_len[:RES], cache)
-    loads["parked"].wait()
-
-    q_recv()
-    parked_q = dot(hot_park, q_all[...].reshape(wide, 256))
-    park_a, park_m, park_t = cache_attention(
-        jnp.concatenate([parked_q[:RES], parked_q[RES:]], axis=1), park_len, parked)
-
-    a_block = jnp.concatenate([
-        jnp.concatenate(park_a[:2], axis=1), jnp.concatenate(park_a[2:], axis=1)], axis=0).astype(BF16)
-    a_send[...] = a_block
-    a_recv, a_sent = launch(0, NREQ, lambda n: a_send, lambda n: a_all.at[n], a_ss.at[0], a_rs.at[0], ahead)
-    stats = jnp.concatenate(park_m + park_t, axis=0)
-    shape = (2 * NHEAD * RES, HD)
-    stats = jnp.sum(jnp.where(iota(shape, 0) == iota(shape, 1), stats, 0.0), axis=0, keepdims=True)
-    st_send[...] = stats
-    st_recv, st_sent = launch(0, NREQ, lambda n: st_send, lambda n: st_all.at[n], a_ss.at[1], a_rs.at[1], ahead)
-    a_all[NREQ - 1] = a_block
-    st_all[NREQ - 1] = stats
-    q_sent()
-
-    new_score = [SCALE * jnp.sum(q[:, h * HD:(h + 1) * HD] * k[:, h * HD:(h + 1) * HD], axis=1, keepdims=True)
-                 for h in range(NHEAD)]
-
-    def finish(first, a, m, t):
-        pieces = []
-        for h in range(NHEAD):
-            score = new_score[h][first:first + RES]
-            top = jnp.maximum(m[h], score)
-            old = t[h] * jnp.exp(m[h] - top)
-            new = jnp.exp(score - top)
-            total = old + new
-            pieces.append(a[h] * (old / total) + v[first:first + RES, h * HD:(h + 1) * HD] * (new / total))
-        out = dot(jnp.concatenate(pieces, axis=1).astype(BF16), wo[...])
-        return jnp.concatenate([out[:, :1024], out[:, 1024:]], axis=0).astype(BF16)
-
-    def summed(parts):
-        whole = (parts[0].astype(F32) + parts[1].astype(F32)) + (parts[2].astype(F32) + parts[3].astype(F32))
-        return jnp.concatenate([whole[:RES], whole[RES:]], axis=1)
-
-    loads["wo"].wait()
-    home_all[head] = finish(0, home_a, home_m, home_t)
-    home_recv, home_sent = head_exchange(lambda p: home_all.at[head], lambda p: home_all.at[p], h_ss.at[0], h_rs.at[0])
-
     loads["ids"].wait()
     ids = ids_ref[...]
     expert = iota((E, ROWS), 0)
@@ -280,6 +235,57 @@
     low_half = (g_col % ROWS) // RES == 0
     taken_halves = jnp.concatenate([jnp.where(low_half, taken, 0.0), jnp.where(low_half, 0.0, taken)], axis=0)
     taken_t = taken_halves.T.astype(BF16)
+    pl.semaphore_wait(barrier, NREQ - 1 + NHEAD - 1)
+    q_recv, q_sent = launch(0, NREQ, lambda n: q_send, lambda n: q_all.at[n], q_ss.at[0], q_rs.at[0], ahead)
+
+    loads["wk"].wait()
+    k = round_trip(rotate(dot(normed, wk[...]), cosine, sine))
+    loads["wv"].wait()
+    v = round_trip(dot(normed, wv[...]))
+    loads["cache"].wait()
+    home_a, home_m, home_t = cache_attention(q[:RES], own_len[:RES], cache)
+    new_score = [SCALE * jnp.sum(q[:, h * HD:(h + 1) * HD] * k[:, h * HD:(h + 1) * HD], axis=1, keepdims=True)
+                 for h in range(NHEAD)]
+
+    def finish(first, a, m, t):
+        pieces = []
+        for h in range(NHEAD):
+            score = new_score[h][first:first + RES]
+            top = jnp.maximum(m[h], score)
+            old = t[h] * jnp.exp(m[h] - top)
+            new = jnp.exp(score - top)
+            total = old + new
+            pieces.append(a[h] * (old / total) + v[first:first + RES, h * HD:(h + 1) * HD] * (new / total))
+        out = dot(jnp.concatenate(pieces, axis=1).astype(BF16), wo[...])
+        return jnp.concatenate([out[:, :1024], out[:, 1024:]], axis=0).astype(BF16)
+
+    def summed(parts):
+        whole = (parts[0].astype(F32) + parts[1].astype(F32)) + (parts[2].astype(F32) + parts[3].astype(F32))
+        return jnp.concatenate([whole[:RES], whole[RES:]], axis=1)
+
+    loads["wo"].wait()
+    home_all[head] = finish(0, home_a, home_m, home_t)
+    home_recv, home_sent = head_exchange(lambda p: home_all.at[head], lambda p: home_all.at[p], h_ss.at[0], h_rs.at[0])
+    loads["parked"].wait()
+
+    q_recv()
+    parked_q = dot(hot_park, q_all[...].reshape(wide, 256))
+    park_a, park_m, park_t = cache_attention(
+        jnp.concatenate([parked_q[:RES], parked_q[RES:]], axis=1), park_len, parked)
+
+    a_block = jnp.concatenate([
+        jnp.concatenate(park_a[:2], axis=1), jnp.concatenate(park_a[2:], axis=1)], axis=0).astype(BF16)
+    a_send[...] = a_block
+    a_recv, a_sent = launch(0, NREQ, lambda n: a_send, lambda n: a_all.at[n], a_ss.at[0], a_rs.at[0], ahead)
+    stats = jnp.concatenate(park_m + park_t, axis=0)
+    shape = (2 * NHEAD * RES, HD)
+    stats = jnp.sum(jnp.where(iota(shape, 0) == iota(shape, 1), stats, 0.0), axis=0, keepdims=True)
+    st_send[...] = stats
+    st_recv, st_sent = launch(0, NREQ, lambda n: st_send, lambda n: st_all.at[n], a_ss.at[1], a_rs.at[1], ahead)
+    a_all[NREQ - 1] = a_block
+    st_all[NREQ - 1] = stats
+    q_sent()
+
     loads["gain_m"].wait()
     home_recv()
     home_residual = hidden[:RES] + summed(home_all)
@@ -307,16 +313,15 @@
     residual = jnp.concatenate([home_residual, hidden[RES:] + summed(back_all)], axis=0)
     normed_f = round_trip(rms_scale(residual, gain_m_ref[...]))
 
-    stacked = jnp.concatenate([normed_f[:, :1024], normed_f[:, 1024:]], axis=0).astype(BF16)
+    stacked = jnp.concatenate(split(normed_f), axis=0).astype(BF16)
     disp[...] = dot(taken_t, stacked).astype(BF16).reshape(NREQ, ROWS, 1024)
     def quarter(p):
         return pl.ds(pl.multiple_of(p * 256, 256), 256)
 
-    far = GROUPS[0][1]
-    moves = [launch(0, far, lambda n: disp.at[n, :, quarter(head)], lambda n: arrived.at[n, :, quarter(head)],
-                    d_ss.at[0], d_rs.at[0], ahead)]
-    for g, (lo, hi) in list(enumerate(GROUPS))[1:]:
-        moves.append(launch(lo, hi, lambda n: disp.at[n], lambda n: arrived.at[n], d_ss.at[g], d_rs.at[g], ahead))
+    far_moves = [launch(lo, hi, lambda n: disp.at[n, :, quarter(head)], lambda n: arrived.at[n, :, quarter(head)],
+                        d_ss.at[g], d_rs.at[g], ahead) for g, (lo, hi) in enumerate(FAR)]
+    moves = [launch(lo, hi, lambda n: disp.at[n], lambda n: arrived.at[n], d_ss.at[2 + g], d_rs.at[2 + g], ahead)
+             for g, (lo, hi) in enumerate(NEAR)]
     arrived[NREQ - 1] = disp[NREQ - 1]
     resid[...] = residual
     h_sent()
@@ -341,59 +346,71 @@
     def experts(lo, hi):
         count = hi - lo
         tokens = arrived[lo:hi].astype(F32).reshape(count, 2, RES, 1024)
-        left = tokens[:, 0].reshape(count * RES, 1024).astype(BF16)
-        right = tokens[:, 1].reshape(count * RES, 1024).astype(BF16)
+        tokens = join(tokens[:, 0].reshape(count * RES, 1024), tokens[:, 1].reshape(count * RES, 1024)).astype(BF16)
         which = (iota((count * RES, FFL), 0) % RES) // 4
         inner = []
         for e in range(2):
-            gate = dot(left, wg[e, :1024]) + dot(right, wg[e, 1024:])
-            up = dot(left, wu[e, :1024]) + dot(right, wu[e, 1024:])
+            gate = dot(tokens, wg[e])
+            up = dot(tokens, wu[e])
             act = gate / (1.0 + jnp.exp(-gate)) * up
             inner.append(jnp.where(which == e, act, 0.0).astype(BF16))
-        parts = []
-        for half in range(2):
-            cols = slice(half * 1024, (half + 1) * 1024)
-            y = dot(inner[0], wd[0, :, cols]) + dot(inner[1], wd[1, :, cols])
-            parts.append(y.reshape(count, RES, 1024))
-        ret_send[lo:hi] = jnp.concatenate(parts, axis=1).astype(BF16)
+        out = dot(inner[0], wd[0]) + dot(inner[1], wd[1])
+        out = [part.reshape(count, RES, 1024) for part in split(out)]
+        ret_send[lo:hi] = jnp.concatenate(out, axis=1).astype(BF16)
 
     def give_back(g):
-        lo, hi = GROUPS[g]
+        lo, hi = NEAR[g]
         return launch(lo, hi, lambda n: ret_send.at[n], lambda n: ret.at[n], r_ss.at[g], r_rs.at[g], behind)
 
-    moves[0][0]()
-    y_recv, y_sent = head_exchange(
-        lambda p: arrived.at[pl.ds(0, far), :, quarter(head)],
-        lambda p: arrived.at[pl.ds(0, far), :, quarter(p)], y_ss, y_rs)
-    moves[1][0]()
-    experts(*GROUPS[1])
-    returns = [give_back(1)]
-    moves[2][0]()
-    experts(*GROUPS[2])
+    swaps = []
+    for g, (lo, hi) in enumerate(FAR):
+        far_moves[g][0]()
+        swaps.append(head_exchange(
+            lambda p: arrived.at[pl.ds(lo, hi - lo), :, quarter(head)],
+            lambda p: arrived.at[pl.ds(lo, hi - lo), :, quarter(p)], y_ss.at[g], y_rs.at[g]))
+    returns = []
+    for g, (lo, hi) in enumerate(NEAR):
+        moves[g][0]()
+        experts(lo, hi)
+        returns.append(give_back(g))
     ret[NREQ - 1] = ret_send[NREQ - 1]
-    y_recv()
-    experts(*GROUPS[0])
-    returns.append(give_back(0))
-    returns.append(give_back(2))
-    y_sent()
-    for move in moves:
-        move[1]()
+    parts = []
+    for g, (lo, hi) in enumerate(FAR):
+        swaps[g][0]()
+        experts(lo, hi)
+        parts.append(head_exchange(
+            lambda p: ret_send.at[pl.ds(lo, hi - lo), :, quarter(p)],
+            lambda p: part_all.at[p, pl.ds(lo, hi - lo)], p_ss.at[g], p_rs.at[g]))
+        part_all[head, lo:hi] = ret_send[lo:hi, :, quarter(head)]
+    far_returns = []
+    for g, (lo, hi) in enumerate(FAR):
+        parts[g][0]()
+        whole = [part_all[h, lo:hi].astype(F32) for h in range(NHEAD)]
+        far_send[lo:hi] = ((whole[0] + whole[1]) + (whole[2] + whole[3])).astype(BF16)
+        far_returns.append(launch(
+            lo, hi, lambda n: far_send.at[n], lambda n: far_ret.at[n], t_ss.at[g], t_rs.at[g], behind))
     for back_move in returns:
         back_move[0]()
-    mixed = dot(mix, ret[...].reshape(wide, 1024))
-    mixture = [mixed[0:16] + mixed[16:32], mixed[32:48] + mixed[48:64]]
+    mixed = dot(mix[:, FIRST * ROWS:], ret[FIRST:].reshape(wide - FIRST * ROWS, 1024))
+    mixture = join(mixed[0:16] + mixed[16:32], mixed[32:48] + mixed[48:64])
     for h in range(NHEAD):
-        fin_send[h] = mixture[h // 2][:, (h % 2) * WIDTH:(h % 2 + 1) * WIDTH].astype(BF16)
+        fin_send[h] = mixture[:, h * WIDTH:(h + 1) * WIDTH].astype(BF16)
     f_recv, f_sent = head_exchange(lambda p: fin_send.at[p], lambda p: fin_all.at[p], f_ss, f_rs)
     fin_all[head] = fin_send[head]
-    for back_move in returns:
-        back_move[1]()
+    for group in swaps + parts + far_moves + moves + returns:
+        group[1]()
     own = resid[:, pl.ds(pl.multiple_of(head * WIDTH, WIDTH), WIDTH)]
     f_recv()
     total = own + ((fin_all[0].astype(F32) + fin_all[1].astype(F32))
                    + (fin_all[2].astype(F32) + fin_all[3].astype(F32)))
+    for group in far_returns:
+        group[0]()
+    mixed = dot(mix[:, :FIRST * ROWS], far_ret[...].reshape(FIRST * ROWS, 256))
+    total = total + jnp.concatenate([mixed[0:16] + mixed[16:32], mixed[32:48] + mixed[48:64]], axis=1)
     out_ref[...] = total.astype(BF16)
     f_sent()
+    for group in far_returns:
+        group[1]()
 
 
 def body(hidden_in, gain_attn, gain_moe, w_query, w_key, w_value, w_out, w_router, w_gate, w_up, w_down,
@@ -423,13 +440,15 @@
             pltpu.VMEM((NHEAD, ROWS, 1024), BF16), pltpu.VMEM((NHEAD, ROWS, 1024), BF16),
             pltpu.VMEM(wide, BF16), pltpu.VMEM(wide, BF16),
             pltpu.VMEM(wide, BF16), pltpu.VMEM(wide, BF16),
+            pltpu.VMEM((NHEAD, FIRST, ROWS, 256), BF16),
+            pltpu.VMEM((FIRST, ROWS, 256), BF16), pltpu.VMEM((FIRST, ROWS, 256), BF16),
             pltpu.VMEM((NHEAD, ROWS, WIDTH), BF16), pltpu.VMEM((NHEAD, ROWS, WIDTH), BF16),
             pltpu.VMEM((ROWS, D), F32),
             dma((len(operands),)),
             dma((1,)), dma((1,)), dma((2,)), dma((2,)),
             dma((2, NHEAD)), dma((2, NHEAD)),
-            dma((len(GROUPS),)), dma((len(GROUPS),)), dma((NHEAD,)), dma((NHEAD,)),
-            dma((len(GROUPS),)), dma((len(GROUPS),)),
+            dma((4,)), dma((4,)), dma((2, NHEAD)), dma((2, NHEAD)), dma((2, NHEAD)), dma((2, NHEAD)),
+            dma((2,)), dma((2,)), dma((2,)), dma((2,)),
             dma((NHEAD,)), dma((NHEAD,)),
         ],
         compiler_params=pltpu.CompilerParams(

time: 56.1 us -> 53.2 us (0.948)
  Pallas kernels: 54.5 us -> 51.7 us
    pallas_call x1, Pallas kernels: 54.5 us -> 51.7 us  [body(): pl.pallas_call(kernel, out_shape=jax.ShapeDtypeStruct((ROWS, WIDTH), BF16...]
where the time goes in v4:
time: 53.2 us; the launch traced here: 53 us
  Pallas kernels  51.7 us (97%)
  local copies, waits for them, and re-layouts  1.32 us (2%)
    pallas_call x1, Pallas kernels, body(): pl.pallas_call(kernel, out_shape=jax.ShapeDtypeStruct((ROWS, WIDTH), BF16...  51.7 us
    unnamed x1, local copies, waits for them, and re-layouts  1.32 us

profile of v4, /device:TPU:1, one launch (start us, length us, event | category | flops | bytes accessed | tf_op | source)
XLA Modules:
  0.0 53.0 jit_solution(773985887436471627)
XLA Ops:
  0.0 51.7 %shard_map.163 = bf16[16,512]{1,0:T(8,128)(2,1)} custom-call(bf16[16,2048]{1,0:T(8,128)(2,1)} %hidden_hbm.1, f32[1,2048]{1,0:T(1,128)} %bitcast.7, f32[1,2048]{1,0:T(1,128)} %bitcast.8, f32[8,512]{1,0:T(8,128)} %constant.2.clone.table_hbm, s32[1,512]{1,0:T(1,128)} %bitcast.10, s32[1,256]{1,0:T(1,128)} %bitcast.11, s32[8,16]{1,0:T(8,128)} %bitcast.9, ...), custom_call_target="tpu_custom_call" | custom-call | tf_op jit(solution)/shard_map/pallas_call | solution.py:431
  51.7 1.3 %copy.19 = bf16[16,512]{1,0:T(8,128)(2,1)} copy(bf16[16,512]{1,0:T(8,128)(2,1)} %shard_map.163) | data formatting | bytes 32768

commit v5 on v4

--- a/solution.py
+++ b/solution.py
@@ -73,7 +73,7 @@
     return jnp.concatenate(parts, axis=1)
 
 
-def cache_attention(q, row_lengths, kv):
+def cache_attention(q, row_lengths, kv, early=None):
     stacked = jnp.concatenate([q] * NHEAD, axis=0)
     row = iota((NHEAD * RES, WIDTH), 0)
     col = iota((NHEAD * RES, WIDTH), 1)
@@ -90,6 +90,8 @@
     row_max = jnp.max(scores, axis=1, keepdims=True)
     weights = jnp.where(usable, jnp.exp(scores - row_max), 0.0)
     row_total = jnp.sum(weights, axis=1, keepdims=True)
+    if early is not None:
+        early(row_max, row_total)
     probs = weights.astype(BF16)
     pieces = [jnp.zeros((RES, HD), F32)] * NHEAD
     small = iota((RES, HD), 0)
@@ -217,6 +219,68 @@
     hot_block = (jnp.floor(own_source[:RES] / RES) == block_src.astype(F32)).astype(F32).astype(BF16)
     hot_home = (same_half & (own_source == place.astype(F32))).astype(F32).astype(BF16)
 
+    pl.semaphore_wait(barrier, NREQ - 1 + NHEAD - 1)
+    q_recv, q_sent = launch(0, NREQ, lambda n: q_send, lambda n: q_all.at[n], q_ss.at[0], q_rs.at[0], ahead)
+
+    loads["wk"].wait()
+    k = round_trip(rotate(dot(normed, wk[...]), cosine, sine))
+    loads["wv"].wait()
+    v = round_trip(dot(normed, wv[...]))
+    loads["cache"].wait()
+    home_a, home_m, home_t = cache_attention(q[:RES], own_len[:RES], cache)
+    new_score = [SCALE * jnp.sum(q[:, h * HD:(h + 1) * HD] * k[:, h * HD:(h + 1) * HD], axis=1, keepdims=True)
+                 for h in range(NHEAD)]
+
+    def merge_weights(first, m, t):
+        pairs = []
+        for h in range(NHEAD):
+            score = new_score[h][first:first + RES]
+            top = jnp.maximum(m[h], score)
+            old = t[h] * jnp.exp(m[h] - top)
+            new = jnp.exp(score - top)
+            total = old + new
+            pairs.append((jnp.broadcast_to(old / total, (RES, HD)),
+                          v[first:first + RES, h * HD:(h + 1) * HD] * (new / total)))
+        return pairs
+
+    def finish(pairs, a):
+        pieces = [a[h] * pairs[h][0] + pairs[h][1] for h in range(NHEAD)]
+        out = dot(jnp.concatenate(pieces, axis=1).astype(BF16), wo[...])
+        return jnp.concatenate([out[:, :1024], out[:, 1024:]], axis=0).astype(BF16)
+
+    def summed(parts):
+        whole = (parts[0].astype(F32) + parts[1].astype(F32)) + (parts[2].astype(F32) + parts[3].astype(F32))
+        return jnp.concatenate([whole[:RES], whole[RES:]], axis=1)
+
+    loads["wo"].wait()
+    home_all[head] = finish(merge_weights(0, home_m, home_t), home_a)
+    home_recv, home_sent = head_exchange(lambda p: home_all.at[head], lambda p: home_all.at[p], h_ss.at[0], h_rs.at[0])
+    loads["parked"].wait()
+
+    q_recv()
+    parked_q = dot(hot_park, q_all[...].reshape(wide, 256))
+    stat_moves = []
+
+    def send_stats(row_max, row_total):
+        stats = jnp.concatenate([row_max, row_total], axis=0)
+        shape = (2 * NHEAD * RES, HD)
+        stats = jnp.sum(jnp.where(iota(shape, 0) == iota(shape, 1), stats, 0.0), axis=0, keepdims=True)
+        st_send[...] = stats
+        st_all[NREQ - 1] = stats
+        stat_moves.extend(launch(
+            0, NREQ, lambda n: st_send, lambda n: st_all.at[n], a_ss.at[1], a_rs.at[1], ahead))
+
+    park_a, park_m, park_t = cache_attention(
+        jnp.concatenate([parked_q[:RES], parked_q[RES:]], axis=1), park_len, parked, send_stats)
+    st_recv, st_sent = stat_moves
+
+    a_block = jnp.concatenate([
+        jnp.concatenate(park_a[:2], axis=1), jnp.concatenate(park_a[2:], axis=1)], axis=0).astype(BF16)
+    a_send[...] = a_block
+    a_recv, a_sent = launch(0, NREQ, lambda n: a_send, lambda n: a_all.at[n], a_ss.at[0], a_rs.at[0], ahead)
+    a_all[NREQ - 1] = a_block
+    q_sent()
+
     loads["ids"].wait()
     ids = ids_ref[...]
     expert = iota((E, ROWS), 0)
@@ -235,63 +299,10 @@
     low_half = (g_col % ROWS) // RES == 0
     taken_halves = jnp.concatenate([jnp.where(low_half, taken, 0.0), jnp.where(low_half, 0.0, taken)], axis=0)
     taken_t = taken_halves.T.astype(BF16)
-    pl.semaphore_wait(barrier, NREQ - 1 + NHEAD - 1)
-    q_recv, q_sent = launch(0, NREQ, lambda n: q_send, lambda n: q_all.at[n], q_ss.at[0], q_rs.at[0], ahead)
-
-    loads["wk"].wait()
-    k = round_trip(rotate(dot(normed, wk[...]), cosine, sine))
-    loads["wv"].wait()
-    v = round_trip(dot(normed, wv[...]))
-    loads["cache"].wait()
-    home_a, home_m, home_t = cache_attention(q[:RES], own_len[:RES], cache)
-    new_score = [SCALE * jnp.sum(q[:, h * HD:(h + 1) * HD] * k[:, h * HD:(h + 1) * HD], axis=1, keepdims=True)
-                 for h in range(NHEAD)]
-
-    def finish(first, a, m, t):
-        pieces = []
-        for h in range(NHEAD):
-            score = new_score[h][first:first + RES]
-            top = jnp.maximum(m[h], score)
-            old = t[h] * jnp.exp(m[h] - top)
-            new = jnp.exp(score - top)
-            total = old + new
-            pieces.append(a[h] * (old / total) + v[first:first + RES, h * HD:(h + 1) * HD] * (new / total))
-        out = dot(jnp.concatenate(pieces, axis=1).astype(BF16), wo[...])
-        return jnp.concatenate([out[:, :1024], out[:, 1024:]], axis=0).astype(BF16)
-
-    def summed(parts):
-        whole = (parts[0].astype(F32) + parts[1].astype(F32)) + (parts[2].astype(F32) + parts[3].astype(F32))
-        return jnp.concatenate([whole[:RES], whole[RES:]], axis=1)
-
-    loads["wo"].wait()
-    home_all[head] = finish(0, home_a, home_m, home_t)
-    home_recv, home_sent = head_exchange(lambda p: home_all.at[head], lambda p: home_all.at[p], h_ss.at[0], h_rs.at[0])
-    loads["parked"].wait()
-
-    q_recv()
-    parked_q = dot(hot_park, q_all[...].reshape(wide, 256))
-    park_a, park_m, park_t = cache_attention(
-        jnp.concatenate([parked_q[:RES], parked_q[RES:]], axis=1), park_len, parked)
-
-    a_block = jnp.concatenate([
-        jnp.concatenate(park_a[:2], axis=1), jnp.concatenate(park_a[2:], axis=1)], axis=0).astype(BF16)
-    a_send[...] = a_block
-    a_recv, a_sent = launch(0, NREQ, lambda n: a_send, lambda n: a_all.at[n], a_ss.at[0], a_rs.at[0], ahead)
-    stats = jnp.concatenate(park_m + park_t, axis=0)
-    shape = (2 * NHEAD * RES, HD)
-    stats = jnp.sum(jnp.where(iota(shape, 0) == iota(shape, 1), stats, 0.0), axis=0, keepdims=True)
-    st_send[...] = stats
-    st_recv, st_sent = launch(0, NREQ, lambda n: st_send, lambda n: st_all.at[n], a_ss.at[1], a_rs.at[1], ahead)
-    a_all[NREQ - 1] = a_block
-    st_all[NREQ - 1] = stats
-    q_sent()
-
     loads["gain_m"].wait()
     home_recv()
     home_residual = hidden[:RES] + summed(home_all)
 
-    a_recv()
-    back = dot(hot_home, a_all[...].reshape(wide, 256))
     st_recv()
     st = st_all[...].reshape(NREQ, HD)
     st0 = round_trip(st)
@@ -302,8 +313,12 @@
     turn = own_source[:RES] - jnp.floor(own_source[:RES] / RES) * RES
     back_s = [jnp.sum(jnp.where(lane == turn + n * RES, picked, 0.0), axis=1, keepdims=True)
               for n in range(2 * NHEAD)]
+    back_pairs = merge_weights(RES, back_s[:NHEAD], back_s[NHEAD:])
+
+    a_recv()
+    back = dot(hot_home, a_all[...].reshape(wide, 256))
     back_a = [back[(h // 2) * RES:(h // 2 + 1) * RES, (h % 2) * HD:(h % 2 + 1) * HD] for h in range(NHEAD)]
-    back_all[head] = finish(RES, back_a, back_s[:NHEAD], back_s[NHEAD:])
+    back_all[head] = finish(back_pairs, back_a)
     h_recv, h_sent = head_exchange(lambda p: back_all.at[head], lambda p: back_all.at[p], h_ss.at[1], h_rs.at[1])
     a_sent()
     st_sent()

time: 53.2 us -> 52.6 us (0.989)
  Pallas kernels: 51.7 us -> 51.1 us
    pallas_call x1, Pallas kernels: 51.7 us -> 51.1 us  [body(): pl.pallas_call(kernel, out_shape=jax.ShapeDtypeStruct((ROWS, WIDTH), BF16...]
where the time goes in v5:
time: 52.6 us; the launch traced here: 52.4 us
  Pallas kernels  51.1 us (97%)
  local copies, waits for them, and re-layouts  1.32 us (3%)
    pallas_call x1, Pallas kernels, body(): pl.pallas_call(kernel, out_shape=jax.ShapeDtypeStruct((ROWS, WIDTH), BF16...  51.1 us
    unnamed x1, local copies, waits for them, and re-layouts  1.32 us

profile of v5, /device:TPU:1, one launch (start us, length us, event | category | flops | bytes accessed | tf_op | source)
XLA Modules:
  0.0 52.4 jit_solution(14784814372340200358)
XLA Ops:
  0.0 51.1 %shard_map.163 = bf16[16,512]{1,0:T(8,128)(2,1)} custom-call(bf16[16,2048]{1,0:T(8,128)(2,1)} %hidden_hbm.1, f32[1,2048]{1,0:T(1,128)} %bitcast.7, f32[1,2048]{1,0:T(1,128)} %bitcast.8, f32[8,512]{1,0:T(8,128)} %constant.2.clone.table_hbm, s32[1,512]{1,0:T(1,128)} %bitcast.10, s32[1,256]{1,0:T(1,128)} %bitcast.11, s32[8,16]{1,0:T(8,128)} %bitcast.9, ...), custom_call_target="tpu_custom_call" | custom-call | tf_op jit(solution)/shard_map/pallas_call | solution.py:446
  51.1 1.3 %copy.19 = bf16[16,512]{1,0:T(8,128)(2,1)} copy(bf16[16,512]{1,0:T(8,128)(2,1)} %shard_map.163) | data formatting | bytes 32768

commit v6 on v5

--- a/solution.py
+++ b/solution.py
@@ -31,7 +31,7 @@
 OFFSETS = sorted(
     ((dx, dz, dc) for dx in range(4) for dz in range(4) for dc in range(2)),
     key=lambda o: (-(ring(o[0]) + ring(o[1])), -o[2], abs(o[0] - o[1]), o))
-FAR = ((0, 6), (6, 10))
+FAR = ((0, 4), (4, 10))
 NEAR = ((10, 22), (22, 32))
 FIRST = 10
 EPS = 1e-06
@@ -252,9 +252,6 @@
         whole = (parts[0].astype(F32) + parts[1].astype(F32)) + (parts[2].astype(F32) + parts[3].astype(F32))
         return jnp.concatenate([whole[:RES], whole[RES:]], axis=1)
 
-    loads["wo"].wait()
-    home_all[head] = finish(merge_weights(0, home_m, home_t), home_a)
-    home_recv, home_sent = head_exchange(lambda p: home_all.at[head], lambda p: home_all.at[p], h_ss.at[0], h_rs.at[0])
     loads["parked"].wait()
 
     q_recv()
@@ -280,6 +277,10 @@
     a_recv, a_sent = launch(0, NREQ, lambda n: a_send, lambda n: a_all.at[n], a_ss.at[0], a_rs.at[0], ahead)
     a_all[NREQ - 1] = a_block
     q_sent()
+
+    loads["wo"].wait()
+    home_all[head] = finish(merge_weights(0, home_m, home_t), home_a)
+    home_recv, home_sent = head_exchange(lambda p: home_all.at[head], lambda p: home_all.at[p], h_ss.at[0], h_rs.at[0])
 
     loads["ids"].wait()
     ids = ids_ref[...]
@@ -329,12 +330,13 @@
     normed_f = round_trip(rms_scale(residual, gain_m_ref[...]))
 
     stacked = jnp.concatenate(split(normed_f), axis=0).astype(BF16)
-    disp[...] = dot(taken_t, stacked).astype(BF16).reshape(NREQ, ROWS, 1024)
+    disp[:FIRST] = dot(taken_t[:FIRST * ROWS], stacked).astype(BF16).reshape(FIRST, ROWS, 1024)
     def quarter(p):
         return pl.ds(pl.multiple_of(p * 256, 256), 256)
 
     far_moves = [launch(lo, hi, lambda n: disp.at[n, :, quarter(head)], lambda n: arrived.at[n, :, quarter(head)],
                         d_ss.at[g], d_rs.at[g], ahead) for g, (lo, hi) in enumerate(FAR)]
+    disp[FIRST:] = dot(taken_t[FIRST * ROWS:], stacked).astype(BF16).reshape(NREQ - FIRST, ROWS, 1024)
     moves = [launch(lo, hi, lambda n: disp.at[n], lambda n: arrived.at[n], d_ss.at[2 + g], d_rs.at[2 + g], ahead)
              for g, (lo, hi) in enumerate(NEAR)]
     arrived[NREQ - 1] = disp[NREQ - 1]
@@ -384,11 +386,14 @@
             lambda p: arrived.at[pl.ds(lo, hi - lo), :, quarter(head)],
             lambda p: arrived.at[pl.ds(lo, hi - lo), :, quarter(p)], y_ss.at[g], y_rs.at[g]))
     returns = []
-    for g, (lo, hi) in enumerate(NEAR):
+
+    def near(g):
+        lo, hi = NEAR[g]
         moves[g][0]()
         experts(lo, hi)
         returns.append(give_back(g))
-    ret[NREQ - 1] = ret_send[NREQ - 1]
+
+    near(0)
     parts = []
     for g, (lo, hi) in enumerate(FAR):
         swaps[g][0]()
@@ -397,6 +402,8 @@
             lambda p: ret_send.at[pl.ds(lo, hi - lo), :, quarter(p)],
             lambda p: part_all.at[p, pl.ds(lo, hi - lo)], p_ss.at[g], p_rs.at[g]))
         part_all[head, lo:hi] = ret_send[lo:hi, :, quarter(head)]
+    near(1)
+    ret[NREQ - 1] = ret_send[NREQ - 1]
     far_returns = []
     for g, (lo, hi) in enumerate(FAR):
         parts[g][0]()

time: 52.6 us -> 52.1 us (level)
  no operation moved by 1% of the time
where the time goes in v6:
time: 52.1 us; the launch traced here: 52 us
  Pallas kernels  50.6 us (97%)
  local copies, waits for them, and re-layouts  1.32 us (3%)
    pallas_call x1, Pallas kernels, body(): pl.pallas_call(kernel, out_shape=jax.ShapeDtypeStruct((ROWS, WIDTH), BF16...  50.6 us
    unnamed x1, local copies, waits for them, and re-layouts  1.32 us

profile of v6, /device:TPU:1, one launch (start us, length us, event | category | flops | bytes accessed | tf_op | source)
XLA Modules:
  0.0 52.0 jit_solution(5879745657694104878)
XLA Ops:
  0.0 50.6 %shard_map.163 = bf16[16,512]{1,0:T(8,128)(2,1)} custom-call(bf16[16,2048]{1,0:T(8,128)(2,1)} %hidden_hbm.1, f32[1,2048]{1,0:T(1,128)} %bitcast.7, f32[1,2048]{1,0:T(1,128)} %bitcast.8, f32[8,512]{1,0:T(8,128)} %constant.2.clone.table_hbm, s32[1,512]{1,0:T(1,128)} %bitcast.10, s32[1,256]{1,0:T(1,128)} %bitcast.11, s32[8,16]{1,0:T(8,128)} %bitcast.9, ...), custom_call_target="tpu_custom_call" | custom-call | tf_op jit(solution)/shard_map/pallas_call | solution.py:453
  50.6 1.3 %copy.19 = bf16[16,512]{1,0:T(8,128)(2,1)} copy(bf16[16,512]{1,0:T(8,128)(2,1)} %shard_map.163) | data formatting | bytes 32768

commit v7 on v6

--- a/solution.py
+++ b/solution.py
@@ -32,7 +32,7 @@
     ((dx, dz, dc) for dx in range(4) for dz in range(4) for dc in range(2)),
     key=lambda o: (-(ring(o[0]) + ring(o[1])), -o[2], abs(o[0] - o[1]), o))
 FAR = ((0, 4), (4, 10))
-NEAR = ((10, 22), (22, 32))
+NEAR = ((10, 26), (26, 32))
 FIRST = 10
 EPS = 1e-06
 

time: 52.1 us -> 52 us (level)
  no operation moved by 1% of the time
where the time goes in v7:
time: 52 us; the launch traced here: 51.8 us
  Pallas kernels  50.5 us (97%)
  local copies, waits for them, and re-layouts  1.32 us (3%)
    pallas_call x1, Pallas kernels, body(): pl.pallas_call(kernel, out_shape=jax.ShapeDtypeStruct((ROWS, WIDTH), BF16...  50.5 us
    unnamed x1, local copies, waits for them, and re-layouts  1.32 us

profile of v7, /device:TPU:1, one launch (start us, length us, event | category | flops | bytes accessed | tf_op | source)
XLA Modules:
  0.0 51.8 jit_solution(4655720739205901386)
XLA Ops:
  0.0 50.5 %shard_map.163 = bf16[16,512]{1,0:T(8,128)(2,1)} custom-call(bf16[16,2048]{1,0:T(8,128)(2,1)} %hidden_hbm.1, f32[1,2048]{1,0:T(1,128)} %bitcast.7, f32[1,2048]{1,0:T(1,128)} %bitcast.8, f32[8,512]{1,0:T(8,128)} %constant.2.clone.table_hbm, s32[1,512]{1,0:T(1,128)} %bitcast.10, s32[1,256]{1,0:T(1,128)} %bitcast.11, s32[8,16]{1,0:T(8,128)} %bitcast.9, ...), custom_call_target="tpu_custom_call" | custom-call | tf_op jit(solution)/shard_map/pallas_call | solution.py:453
  50.5 1.3 %copy.19 = bf16[16,512]{1,0:T(8,128)(2,1)} copy(bf16[16,512]{1,0:T(8,128)(2,1)} %shard_map.163) | data formatting | bytes 32768
